TPU v7x, 32 devices: a whole 2x2x4 slice. The times are simulated.
32 devices in a mesh: dp: 4 (over y, core), ctx: 8 (over z, x).
Axes of the slice: x: 2, y: 2, z: 4, core: 2. Of those that a mesh axis runs over, the one named last changes fastest.
Arguments:
- queries: bfloat16 [4, 8192, 1024], P('dp', 'ctx'), may hold values from -160 to 160
- keys: bfloat16 [4, 8192, 1024], P('dp', 'ctx'), may hold values from -14 to 14
- values: bfloat16 [4, 8192, 1024], P('dp', 'ctx'), may hold values from -4.5 to 4.5
- cotangent: bfloat16 [4, 8192, 1024], P('dp', 'ctx'), may hold values from -6 to 6
- gain: float32 [1024], replicated, may hold values from 0.1 to 1.9
Outputs:
- attended: bfloat16 [4, 8192, 1024], P('dp', 'ctx')
- grad_queries: bfloat16 [4, 8192, 1024], P('dp', 'ctx')
- grad_keys: bfloat16 [4, 8192, 1024], P('dp', 'ctx')
- grad_values: bfloat16 [4, 8192, 1024], P('dp', 'ctx')
- gain_grad: float32 [1024], replicated
All inputs are finite; a program needn't handle non-finite values.
Results may differ from a plain program's by a relative error of at most 0.019.
The roundings to bfloat16 on the way count: a program that leaves them out, or rounds other values in their place, can miss the bound.
Values may be sent and summed in bfloat16 or wider, within the bound.
No kernel may reach another device: no remote copies, remote signals or barrier semaphores. Data moves between devices by JAX's collectives and lax.ppermute only.
A program may use at most 192 MiB of HBM per device.

v0:
```python
import jax
import jax.numpy as jnp
from jax import lax
from jax.sharding import PartitionSpec as P

H = 8
HD = 128
BLOCK = 128
STRIDE = 1024
SUMMARY = 8


NEG = -1e30


def from_behind(value, axis, steps):
    count = lax.axis_size(axis)
    first, last = (max(0, -steps), min(count, count - steps))
    return lax.ppermute(value, axis, [(source, source + steps) for source in range(first, last)])


def to_rows(block_array):
    batch, blocks, heads, width = block_array.shape
    return block_array.transpose(0, 2, 1, 3).reshape(batch, heads, blocks * width)


def to_blocks(row_array, blocks):
    batch, heads, length = row_array.shape
    return row_array.reshape(batch, heads, blocks, length // blocks).transpose(0, 2, 1, 3)


def per_device(queries, keys, values, cotangent, gain):
    f32 = jnp.float32
    bf16 = jnp.bfloat16
    batch, length, width = queries.shape
    blocks = length // BLOCK
    segs = length // STRIDE
    own_sums = segs * SUMMARY
    ctx_count = lax.axis_size("ctx")
    rank = lax.axis_index("ctx")
    scale = HD ** (-0.5)
    scaled = (queries.astype(f32) * gain).astype(bf16)
    rim_keys, rim_values = from_behind(
        (keys[:, length - BLOCK :], values[:, length - BLOCK :]), "ctx", 1
    )
    own_sum_keys = keys.reshape(batch, segs, STRIDE, width)[:, :, STRIDE - SUMMARY :].reshape(
        batch, own_sums, width
    )
    own_sum_values = values.reshape(batch, segs, STRIDE, width)[:, :, STRIDE - SUMMARY :].reshape(
        batch, own_sums, width
    )
    sum_keys, sum_values = (
        lax.all_gather(own_sum_keys, "ctx", axis=1, tiled=True),
        lax.all_gather(own_sum_values, "ctx", axis=1, tiled=True),
    )
    total_sums = sum_keys.shape[1]
    sum_keys = sum_keys.reshape(batch, total_sums, H, HD)
    sum_values = sum_values.reshape(batch, total_sums, H, HD)
    ext_keys = jnp.concatenate([rim_keys, keys], 1).reshape(batch, blocks + 1, BLOCK, H, HD)
    ext_values = jnp.concatenate([rim_values, values], 1).reshape(batch, blocks + 1, BLOCK, H, HD)
    band_keys = jnp.concatenate([ext_keys[:, :-1], ext_keys[:, 1:]], 2)
    band_values = jnp.concatenate([ext_values[:, :-1], ext_values[:, 1:]], 2)
    query_blocks = scaled.reshape(batch, blocks, BLOCK, H, HD)
    scaled_rows = scaled.reshape(batch, length, H, HD)
    grad_rows = cotangent.reshape(batch, length, H, HD)
    grad_blocks = cotangent.reshape(batch, blocks, BLOCK, H, HD)
    query_index = jnp.arange(BLOCK, dtype=jnp.int32)[:, None]
    key_index = jnp.arange(2 * BLOCK, dtype=jnp.int32)[None, :]
    band = (key_index > query_index) & (key_index <= query_index + BLOCK)
    global_block = rank * blocks + jnp.arange(blocks, dtype=jnp.int32)
    band_mask = band[None] & ((global_block > 0)[:, None, None] | (key_index >= BLOCK)[None])
    band_mask = band_mask[None, :, None]
    slot = jnp.arange(total_sums, dtype=jnp.int32)
    sum_pos = slot // SUMMARY * STRIDE + STRIDE - SUMMARY + slot % SUMMARY
    query_pos = rank * length + jnp.arange(length, dtype=jnp.int32)
    sum_mask = (query_pos[:, None] - sum_pos[None, :] >= BLOCK)[None, None]
    band_scores = (
        jnp.einsum("bnqhd,bnkhd->bnhqk", query_blocks, band_keys, preferred_element_type=f32)
        * scale
    )
    band_scores = jnp.where(band_mask, band_scores, NEG)
    sum_scores = (
        jnp.einsum("bqhd,bshd->bhqs", scaled_rows, sum_keys, preferred_element_type=f32) * scale
    )
    sum_scores = jnp.where(sum_mask, sum_scores, NEG)
    top = jnp.maximum(to_rows(jnp.max(band_scores, -1)), jnp.max(sum_scores, -1))
    band_exp = jnp.where(band_mask, jnp.exp(band_scores - to_blocks(top, blocks)[..., None]), 0.0)
    sum_exp = jnp.where(sum_mask, jnp.exp(sum_scores - top[..., None]), 0.0)
    total = to_rows(jnp.sum(band_exp, -1)) + jnp.sum(sum_exp, -1)
    band_prob = band_exp / to_blocks(total, blocks)[..., None]
    sum_prob = sum_exp / total[..., None]
    band_prob_b = band_prob.astype(bf16)
    sum_prob_b = sum_prob.astype(bf16)
    mixed = jnp.einsum(
        "bnhqk,bnkhd->bnqhd", band_prob_b, band_values, preferred_element_type=f32
    ).reshape(batch, length, H, HD)
    mixed = mixed + jnp.einsum(
        "bhqs,bshd->bqhd", sum_prob_b, sum_values, preferred_element_type=f32
    )
    attended = mixed.reshape(batch, length, width).astype(bf16)
    delta = jnp.sum(
        grad_rows.astype(f32) * attended.reshape(batch, length, H, HD).astype(f32), -1
    ).transpose(0, 2, 1)
    band_dprob = jnp.einsum(
        "bnqhd,bnkhd->bnhqk", grad_blocks, band_values, preferred_element_type=f32
    )
    sum_dprob = jnp.einsum("bqhd,bshd->bhqs", grad_rows, sum_values, preferred_element_type=f32)
    band_ds = (band_prob * (band_dprob - to_blocks(delta, blocks)[..., None]) * scale).astype(bf16)
    sum_ds = (sum_prob * (sum_dprob - delta[..., None]) * scale).astype(bf16)
    band_dv = jnp.einsum("bnhqk,bnqhd->bnkhd", band_prob_b, grad_blocks, preferred_element_type=f32)
    band_dk = jnp.einsum("bnhqk,bnqhd->bnkhd", band_ds, query_blocks, preferred_element_type=f32)
    rim_dk, rim_dv = from_behind((band_dk[:, 0, :BLOCK], band_dv[:, 0, :BLOCK]), "ctx", -1)
    sum_dv = jnp.einsum(
        "bhqs,bqhd->bshd", sum_prob_b, grad_rows, preferred_element_type=f32
    ).reshape(batch, total_sums, width)
    sum_dk = jnp.einsum("bhqs,bqhd->bshd", sum_ds, scaled_rows, preferred_element_type=f32).reshape(
        batch, total_sums, width
    )
    whole_dk, whole_dv = lax.psum((sum_dk, sum_dv), "ctx")
    owned_dk = lax.dynamic_slice_in_dim(whole_dk, rank * own_sums, own_sums, 1)
    owned_dv = lax.dynamic_slice_in_dim(whole_dv, rank * own_sums, own_sums, 1)

    def fold_band(pairs, received, owned):
        later = jnp.concatenate([pairs[:, 1:, :BLOCK], received[:, None]], 1)
        folded = (pairs[:, :, BLOCK:] + later).reshape(batch, segs, STRIDE, width)
        folded = folded.at[:, :, STRIDE - SUMMARY :].add(owned.reshape(batch, segs, SUMMARY, width))
        return folded.reshape(batch, length, width).astype(bf16)

    grad_values = fold_band(band_dv, rim_dv, owned_dv)
    grad_keys = fold_band(band_dk, rim_dk, owned_dk)
    grad_scaled = jnp.einsum(
        "bnhqk,bnkhd->bnqhd", band_ds, band_keys, preferred_element_type=f32
    ).reshape(batch, length, H, HD)
    grad_scaled = grad_scaled + jnp.einsum(
        "bhqs,bshd->bqhd", sum_ds, sum_keys, preferred_element_type=f32
    )
    grad_scaled = grad_scaled.reshape(batch, length, width)
    grad_queries = (grad_scaled * gain).astype(bf16)
    gain_part = jnp.sum(grad_scaled * queries.astype(f32), (0, 1))
    gain_total = lax.psum(gain_part, ("dp", "ctx"))
    token_count = batch * lax.axis_size("dp") * length * ctx_count
    gain_grad = gain_total * token_count ** (-0.5)
    return (attended, grad_queries, grad_keys, grad_values, gain_grad)


def solution(mesh):
    in_specs = (
        P("dp", "ctx", None),
        P("dp", "ctx", None),
        P("dp", "ctx", None),
        P("dp", "ctx", None),
        P(),
    )
    out_specs = (
        P("dp", "ctx", None),
        P("dp", "ctx", None),
        P("dp", "ctx", None),
        P("dp", "ctx", None),
        P(),
    )
    return jax.shard_map(
        per_device, mesh=mesh, in_specs=in_specs, out_specs=out_specs, check_vma=False
    )
```

profile of v0, /device:TPU:0, one launch (start us, length us, event | category | flops | bytes accessed | tf_op | source)
XLA Modules:
  0.0 350.7 jit_solution(11404047810387669585)
XLA Ops:
  7.2 1.8 slice.100
  9.0 4.9 %collective-permute-start = (bf16[1,128,1024]{2,1,0:T(8,128)(2,1)}, bf16[1,128,1024]{2,1,0:T(8,128)(2,1)S(1)}, u32[]{:S(2)}, u32[]{:S(2)}) collective-permute-start(bf16[1,128,1024]{2,1,0:T(8,128)(2,1)} %slice.100), channel_id=1, source_target_pairs={{0,1},{1,2},{2,3},{3,4},{4,5},{5,6},{6,7},{8,9},{9,10},{10,11},{11... | collective-permute-start | bytes 786440 | tf_op jit(solution)/shard_map/ppermute | solution.py:19
  13.9 1.7 slice.103
  15.6 3.4 collective-permute-start.1
  19.1 4.1 %copy.35 = f32[1,1024,1024]{1,2,0:T(8,128)} copy(bf16[1,1024,1024]{2,1,0:T(8,128)(2,1)} %param.12) | data formatting | bytes 6291456 | tf_op jit(solution)/shard_map/convert_element_type | solution.py:102
  23.9 1.9 copy.64
  25.9 3.3 copy.43
  30.1 30.6 %all-gather = bf16[1,1,64,1024]{3,2,1,0:T(8,128)(2,1)S(1)} all-gather(bf16[1,1,8,1024]{3,2,1,0:T(8,128)(2,1)S(1)} %slice.118), channel_id=2, replica_groups=mesh['dp'=4,'ctx'=8] {'ctx'}, dimensions={2}, use_global_device_ids=true | all-gather | bytes 147456 | tf_op jit(solution)/shard_map/all_gather | solution.py:53
  61.6 3.9 %fusion.16 = (f32[8,1024]{1,0:T(8,128)S(1)}, f32[8,1024,64]{1,2,0:T(8,128)}) fusion(pred[1024,64]{0,1:T(8,128)(4,1)S(1)} %subtract_compare_fusion, bf16[64,8,128]{2,1,0:T(8,128)(2,1)S(1)} %bitcast.196, bf16[1024,8,128]{2,1,0:T(8,128)(2,1)} %bitcast.184), kind=kOutput, calls=%fused_computation.36 | convolution fusion | flops 135782400 | bytes 4423680 | tf_op jit(solution)/shard_map/bqhd,bshd->bhqs/dot_general | solution.py:83
  65.5 30.5 %all-gather.1 = bf16[1,1,64,1024]{3,2,1,0:T(8,128)(2,1)S(1)} all-gather(bf16[1,1,8,1024]{3,2,1,0:T(8,128)(2,1)S(1)} %slice.121), channel_id=3, replica_groups=mesh['dp'=4,'ctx'=8] {'ctx'}, dimensions={2}, use_global_device_ids=true | all-gather | bytes 147456 | tf_op jit(solution)/shard_map/all_gather | solution.py:54
  96.1 2.0 copy.70
  98.2 2.1 maximum_bitcast_fusion.6
  103.0 2.9 fusion.2
  106.0 3.2 fusion.4
  109.8 1.4 copy-done.13
  114.3 4.0 %fusion.12 = f32[1,8,128,8,128]{4,2,3,1,0:T(8,128)S(1)} fusion(bf16[1,8,128,8,128]{4,2,3,1,0:T(8,128)(2,1)S(1)} %copy.63, bf16[1,8,128,8,128]{4,2,3,1,0:T(8,128)(2,1)S(1)} %copy.62, f32[8,8,128,256]{3,2,1,0:T(8,128)S(1)} %get-tuple-element.48, f32[8,8,128]{2,1,0:T(8,128)S(1)} %fusion.48, f32[8,8,128]{2,1,0:T(8,128)S(1)} %fusion.49, ...), kind=kOutput, calls=%fused_computation.29 | convolution fusion | flops 557842432 | bytes 17104896 | tf_op jit(solution)/shard_map/bnhqk,bnkhd->bnqhd/dot_general | solution.py:94
  118.4 4.3 %copy.31 = f32[1,8,128,8,128]{4,3,2,1,0:T(8,128)} copy(f32[1,8,128,8,128]{4,2,3,1,0:T(8,128)S(1)} %fusion.12) | data formatting | bytes 8388608 | tf_op jit(solution)/shard_map/bnhqk,bnkhd->bnqhd/transpose | solution.py:94
  122.7 5.4 %copy.33 = f32[1,1024,8,128]{1,3,2,0:T(8,128)} copy(f32[1,1024,8,128]{3,2,1,0:T(8,128)} %bitcast.180) | data formatting | bytes 8388608 | tf_op jit(solution)/shard_map/reshape | solution.py:96
  128.2 9.3 %convolution_bitcast_fusion = f32[1,8,256,8,128]{4,2,3,1,0:T(8,128)} fusion(bf16[8,128,8,128]{3,2,1,0:T(8,128)(2,1)} %bitcast.189, f32[8,8,128,256]{3,2,1,0:T(8,128)} %copy-done.6, f32[8,8,128]{2,1,0:T(8,128)S(1)} %fusion.48, f32[8,8,128]{2,1,0:T(8,128)S(1)} %fusion.49, pred[8,128,256]{2,1,0:T(8,128)(4,1)S(1)} %broadcast_and_fusion), kind=kOutput, calls=%fused_computation.21 | convolution fusion | flops 549453824 | bytes 19202048 | tf_op jit(solution)/shard_map/bnhqk,bnqhd->bnkhd/dot_general | solution.py:110
  137.6 2.7 multiply_reduce_fusion
  140.4 7.1 %fusion.1 = bf16[8,8,128,256]{3,2,1,0:T(8,128)(2,1)S(1)} fusion(f32[8,8,128]{2,1,0:T(8,128)S(1)} %bitcast.202, bf16[1,8,128,8,128]{4,2,3,1,0:T(8,128)(2,1)S(1)} %copy-done.21, bf16[1,8,128,8,128]{4,2,3,1,0:T(8,128)(2,1)} %copy-done.22, bf16[8,128,8,128]{3,2,1,0:T(8,128)(2,1)S(1)} %bitcast.191, f32[8,8,128]{2,1,0:T(8,128)S(1)} %fusion.48, ...), kind=kOutput, calls=%fused_computation.2 | convolution fusion | flops 564133888 | bytes 19234816 | tf_op jit(solution)/shard_map/bnqhd,bnkhd->bnhqk/dot_general | solution.py:104
  148.7 4.5 %convolution_bitcast_fusion.1 = f32[1,8,256,8,128]{2,4,3,1,0:T(8,128)} fusion(bf16[8,128,8,128]{1,3,2,0:T(8,128)(2,1)S(1)} %copy.43, bf16[8,8,128,256]{3,2,1,0:T(8,128)(2,1)S(1)} %fusion.1), kind=kOutput, calls=%fused_computation.22 | convolution fusion | flops 536870912 | bytes 14680064 | tf_op jit(solution)/shard_map/bnhqk,bnqhd->bnkhd/dot_general | solution.py:111
  153.2 4.4 %copy.37 = f32[1,8,128,8,128]{4,3,2,1,0:T(8,128)} copy(f32[1,8,128,8,128]{4,2,3,1,0:T(8,128)S(1)} %fusion.11) | data formatting | bytes 8388608 | tf_op jit(solution)/shard_map/bnhqk,bnkhd->bnqhd/transpose | solution.py:131
  157.6 5.5 %copy.41 = f32[1,1024,8,128]{1,3,2,0:T(8,128)} copy(f32[1,1024,8,128]{3,2,1,0:T(8,128)} %bitcast.181) | data formatting | bytes 8388608 | tf_op jit(solution)/shard_map/reshape | solution.py:133
  163.1 3.5 fusion.34
  166.6 1.4 multiply_convert_fusion.1
  168.8 2.7 bitcast_add_fusion
  171.5 5.6 %copy.42 = f32[1,1024,1024]{2,1,0:T(8,128)} copy(f32[1,1024,1024]{1,2,0:T(8,128)} %bitcast.179) | data formatting | bytes 8388608 | tf_op jit(solution)/shard_map/reshape | solution.py:137
  177.1 4.3 %fusion.6 = (f32[1024]{0:T(1024)S(1)}, bf16[1,1024,1024]{2,1,0:T(8,128)(2,1)}) fusion(f32[1,1024,1024]{2,1,0:T(8,128)} %copy.42, bf16[1,1024,1024]{2,1,0:T(8,128)(2,1)S(1)} %copy-done.4, f32[1024]{0:T(1024)S(1)} %copy-done.24), kind=kLoop, calls=%fused_computation.11 | loop fusion | flops 5241856 | bytes 8396800 | tf_op jit(solution)/shard_map/reduce_sum | solution.py:139
  181.4 1.9 slice_bitcast_fusion
  184.6 1.9 slice_bitcast_fusion.1
  187.7 44.9 %psum.23 = f32[1024]{0:T(1024)S(1)} all-reduce(f32[1024]{0:T(1024)S(1)} %get-tuple-element.41), channel_id=1, replica_groups=mesh['dp'=4,'ctx'=8] {'dp','ctx'}, use_global_device_ids=true, to_apply=%region_8.9 | all-reduce | flops 1024 | bytes 8192 | tf_op jit(solution)/shard_map/psum | solution.py:140
  232.6 2.3 fusion.31
  235.5 4.3 %slice.127 = f32[1,7,128,8,128]{4,2,3,1,0:T(8,128)} slice(f32[1,8,256,8,128]{4,2,3,1,0:T(8,128)} %convolution_bitcast_fusion), slice={[0:1], [1:8], [0:128], [0:8], [0:128]} | slice | bytes 7340032 | tf_op jit(solution)/shard_map/slice | solution.py:124
  239.8 4.4 %slice.123 = f32[1,7,128,8,128]{2,4,3,1,0:T(8,128)} slice(f32[1,8,256,8,128]{2,4,3,1,0:T(8,128)} %convolution_bitcast_fusion.1), slice={[0:1], [1:8], [0:128], [0:8], [0:128]} | slice | bytes 7340032 | tf_op jit(solution)/shard_map/slice | solution.py:124
  244.2 2.5 copy.55
  248.5 4.2 %slice_add_fusion = f32[1,8,128,8,128]{4,2,3,1,0:T(8,128)S(1)} fusion(f32[1,8,256,8,128]{4,2,3,1,0:T(8,128)} %convolution_bitcast_fusion, f32[1,1,128,8,128]{4,2,3,1,0:T(8,128)} %bitcast.59, f32[1,7,128,8,128]{4,2,3,1,0:T(8,128)} %slice.127), kind=kLoop, calls=%fused_computation.12 | loop fusion | flops 2097152 | bytes 12582912 | tf_op jit(solution)/shard_map/add | solution.py:125
  252.7 2.4 copy.50
  255.1 2.0 copy.106
  258.4 6.6 %slice_add_fusion.1 = f32[1,8,128,8,128]{2,4,3,1,0:T(8,128)} fusion(f32[1,8,256,8,128]{2,4,3,1,0:T(8,128)} %convolution_bitcast_fusion.1, f32[1,1,128,8,128]{2,4,3,1,0:T(8,128)} %bitcast.45, f32[1,7,128,8,128]{2,4,3,1,0:T(8,128)} %slice.123), kind=kLoop, calls=%fused_computation.13 | loop fusion | flops 2097152 | bytes 12582912 | tf_op jit(solution)/shard_map/add | solution.py:125
  264.9 5.6 %copy.44 = f32[1,8,128,8,128]{4,3,0,2,1:T(8,128)} copy(f32[1,8,128,8,128]{2,4,3,1,0:T(8,128)} %slice_add_fusion.1) | data formatting | bytes 8388608 | tf_op jit(solution)/shard_map/add | solution.py:125
  270.5 7.0 %copy.107 = f32[1,1024,1024]{2,0,1:T(1,128)} copy(f32[1,1024,1024]{2,0,1:T(1,128)} %bitcast.177) | data formatting | bytes 8388608
  277.6 43.6 %all-reduce.3.cloned.1.call-done = (f32[1,64,1024]{2,0,1:T(1,128)}, f32[1,64,1024]{2,0,1:T(1,128)}) async-done(((f32[1,64,1024]{2,0,1:T(1,128)}, f32[1,64,1024]{2,0,1:T(1,128)}), (f32[1,64,1024]{2,0,1:T(1,128)}, f32[1,64,1024]{2,0,1:T(1,128)})) %all-reduce.3.cloned.1.call-update) | async-done | bytes 524304 | tf_op jit(solution)/shard_map/psum | solution.py:119
  321.2 1.5 fusion.45
  322.7 7.0 %convert_element_type.87 = bf16[1,1024,1024]{2,0,1:T(2,128)(2,1)} convert(f32[1,1024,1024]{2,0,1:T(1,128)} %get-tuple-element.54) | non-fusion elementwise | flops 1048576 | bytes 6291456 | tf_op jit(solution)/shard_map/convert_element_type | solution.py:127
  329.7 4.5 %copy.56 = bf16[1,1024,1024]{2,1,0:T(8,128)(2,1)} copy(bf16[1,1024,1024]{2,0,1:T(2,128)(2,1)} %convert_element_type.87) | data formatting | bytes 4194304
  334.2 4.8 %convert_element_type.88 = bf16[1,1024,1024]{2,0,1:T(2,128)(2,1)} convert(f32[1,1024,1024]{2,0,1:T(1,128)S(1)} %copy-done.2) | non-fusion elementwise | flops 1048576 | bytes 6291456 | tf_op jit(solution)/shard_map/convert_element_type | solution.py:127
  339.1 4.3 %copy.57 = bf16[1,1024,1024]{2,1,0:T(8,128)(2,1)} copy(bf16[1,1024,1024]{2,0,1:T(2,128)(2,1)} %convert_element_type.88) | data formatting | bytes 4194304
  (93 shorter events, 17.4 us)
Async XLA Ops:
  7.2 16.2 %copy-start.3 = (bf16[1,1024,1024]{2,1,0:T(8,128)(2,1)S(1)}, bf16[1,1024,1024]{2,1,0:T(8,128)(2,1)}, u32[]{:S(2)}) copy-start(bf16[1,1024,1024]{2,1,0:T(8,128)(2,1)} %param.9) | copy-start | bytes 6291460
  7.2 16.2 %copy-start.24 = (f32[1024]{0:T(1024)S(1)}, f32[1024]{0:T(1024)}, u32[]{:S(2)}) copy-start(f32[1024]{0:T(1024)} %param.13) | copy-start | bytes 12292
  7.2 314.0 %all-reduce.3.cloned.1.call-start = ((), (), s32[]{:S(2)}) async-start(), calls=%async_computation | async-start | bytes 1048576 | tf_op jit(solution)/shard_map/psum | solution.py:119
  9.0 100.7 %collective-permute-start = (bf16[1,128,1024]{2,1,0:T(8,128)(2,1)}, bf16[1,128,1024]{2,1,0:T(8,128)(2,1)S(1)}, u32[]{:S(2)}, u32[]{:S(2)}) collective-permute-start(bf16[1,128,1024]{2,1,0:T(8,128)(2,1)} %slice.100), channel_id=1, source_target_pairs={{0,1},{1,2},{2,3},{3,4},{4,5},{5,6},{6,7},{8,9},{9,10},{10,11},{11... | collective-permute-start | bytes 786440 | tf_op jit(solution)/shard_map/ppermute | solution.py:19
  15.6 82.6 %collective-permute-start.1 = (bf16[1,128,1024]{2,1,0:T(8,128)(2,1)}, bf16[1,128,1024]{2,1,0:T(8,128)(2,1)S(1)}, u32[]{:S(2)}, u32[]{:S(2)}) collective-permute-start(bf16[1,128,1024]{2,1,0:T(8,128)(2,1)} %slice.103), channel_id=1, source_target_pairs={{0,1},{1,2},{2,3},{3,4},{4,5},{5,6},{6,7},{8,9},{9,10},{10,11},{11... | collective-permute-start | bytes 786440 | tf_op jit(solution)/shard_map/ppermute | solution.py:19
  29.2 66.9 %copy-start.5 = (bf16[1,1024,1024]{2,1,0:T(8,128)(2,1)S(1)}, bf16[1,1024,1024]{2,1,0:T(8,128)(2,1)}, u32[]{:S(2)}) copy-start(bf16[1,1024,1024]{2,1,0:T(8,128)(2,1)} %param.12) | copy-start | bytes 6291460
  102.4 3.5 %copy-start.7 = (bf16[1,8,128,8,128]{4,2,3,1,0:T(8,128)(2,1)}, bf16[1,8,128,8,128]{4,2,3,1,0:T(8,128)(2,1)S(1)}, u32[]{:S(2)}) copy-start(bf16[1,8,128,8,128]{4,2,3,1,0:T(8,128)(2,1)S(1)} %copy.61) | copy-start | bytes 6291460
  103.0 2.9 copy-start.9
  105.9 8.4 %copy-start.6 = (f32[8,8,128,256]{3,2,1,0:T(8,128)}, f32[8,8,128,256]{3,2,1,0:T(8,128)S(1)}, u32[]{:S(2)}) copy-start(f32[8,8,128,256]{3,2,1,0:T(8,128)S(1)} %get-tuple-element.48) | copy-start | bytes 25165828
  106.0 3.2 copy-start.14
  106.0 5.2 %copy-start.13 = (bf16[1,1024,1024]{2,1,0:T(8,128)(2,1)S(1)}, bf16[1,1024,1024]{2,1,0:T(8,128)(2,1)}, u32[]{:S(2)}) copy-start(bf16[1,1024,1024]{2,1,0:T(8,128)(2,1)} %param.11) | copy-start | bytes 6291460
  113.7 4.7 %copy-start.20 = (bf16[1,8,128,8,128]{4,2,3,1,0:T(8,128)(2,1)}, bf16[1,8,128,8,128]{4,2,3,1,0:T(8,128)(2,1)S(1)}, u32[]{:S(2)}) copy-start(bf16[1,8,128,8,128]{4,2,3,1,0:T(8,128)(2,1)S(1)} %copy.63) | copy-start | bytes 6291460
  114.3 4.1 %copy-start.22 = (bf16[1,8,128,8,128]{4,2,3,1,0:T(8,128)(2,1)}, bf16[1,8,128,8,128]{4,2,3,1,0:T(8,128)(2,1)S(1)}, u32[]{:S(2)}) copy-start(bf16[1,8,128,8,128]{4,2,3,1,0:T(8,128)(2,1)S(1)} %copy.62) | copy-start | bytes 6291460
  128.2 9.3 %copy-start.11 = (f32[1,1024,1024]{1,2,0:T(8,128)S(1)}, f32[1,1024,1024]{1,2,0:T(8,128)}, u32[]{:S(2)}) copy-start(f32[1,1024,1024]{1,2,0:T(8,128)} %copy.35) | copy-start | bytes 12582916
  128.2 9.3 %copy-start.12 = (f32[1,1024,8,128]{1,3,2,0:T(8,128)S(1)}, f32[1,1024,8,128]{1,3,2,0:T(8,128)}, u32[]{:S(2)}) copy-start(f32[1,1024,8,128]{1,3,2,0:T(8,128)} %copy.33) | copy-start | bytes 12582916
  128.2 9.4 %copy-start.15 = (f32[8,1024,64]{1,2,0:T(8,128)S(1)}, f32[8,1024,64]{1,2,0:T(8,128)}, u32[]{:S(2)}) copy-start(f32[8,1024,64]{1,2,0:T(8,128)} %get-tuple-element.50) | copy-start | bytes 6291460
  137.6 2.7 copy-start.17
  137.6 2.7 copy-start.21
  140.3 7.1 %copy-start.25 = (f32[1024,8]{0,1:T(8,128)}, f32[1024,8]{0,1:T(8,128)S(1)}, u32[]{:S(2)}) copy-start(f32[1024,8]{0,1:T(8,128)S(1)} %get-tuple-element.51) | copy-start | bytes 98308
  140.3 7.1 %copy-start.8 = (bf16[1,8,128,8,128]{4,2,3,1,0:T(8,128)(2,1)S(1)}, bf16[1,8,128,8,128]{4,2,3,1,0:T(8,128)(2,1)}, u32[]{:S(2)}) copy-start(bf16[1,8,128,8,128]{4,2,3,1,0:T(8,128)(2,1)} %copy-done.7) | copy-start | bytes 6291460
  140.3 7.1 %copy-start.10 = (bf16[1,8,128,8,128]{4,2,3,1,0:T(8,128)(2,1)S(1)}, bf16[1,8,128,8,128]{4,2,3,1,0:T(8,128)(2,1)}, u32[]{:S(2)}) copy-start(bf16[1,8,128,8,128]{4,2,3,1,0:T(8,128)(2,1)} %copy-done.9) | copy-start | bytes 6291460
  157.6 5.6 %copy-start.16 = (f32[8,1024,64]{1,2,0:T(8,128)S(1)}, f32[8,1024,64]{1,2,0:T(8,128)}, u32[]{:S(2)}) copy-start(f32[8,1024,64]{1,2,0:T(8,128)} %get-tuple-element.50) | copy-start | bytes 6291460
  163.1 3.5 copy-start.18
  163.1 3.5 copy-start.26
  166.6 2.2 copy-start.1
  171.5 5.6 %copy-start.4 = (bf16[1,1024,1024]{2,1,0:T(8,128)(2,1)S(1)}, bf16[1,1024,1024]{2,1,0:T(8,128)(2,1)}, u32[]{:S(2)}) copy-start(bf16[1,1024,1024]{2,1,0:T(8,128)(2,1)} %param.9) | copy-start | bytes 6291460
  183.3 65.2 %collective-permute-start.3 = (f32[1,128,8,128]{3,1,2,0:T(8,128)}, f32[1,128,8,128]{3,1,2,0:T(8,128)}, u32[]{:S(2)}, u32[]{:S(2)}) collective-permute-start(f32[1,128,8,128]{3,1,2,0:T(8,128)} %slice_bitcast_fusion), channel_id=1, source_target_pairs={{1,0},{2,1},{3,2},{4,3},{5,4},{6,5},{7,6},{9,8},{10,9},{11,10},{12... | collective-permute-start | bytes 1572872 | tf_op jit(solution)/shard_map/ppermute | solution.py:19
  186.4 71.9 %collective-permute-start.2 = (f32[1,128,8,128]{1,3,2,0:T(8,128)}, f32[1,128,8,128]{1,3,2,0:T(8,128)}, u32[]{:S(2)}, u32[]{:S(2)}) collective-permute-start(f32[1,128,8,128]{1,3,2,0:T(8,128)} %slice_bitcast_fusion.1), channel_id=1, source_target_pairs={{1,0},{2,1},{3,2},{4,3},{5,4},{6,5},{7,6},{9,8},{10,9},{11,10},{12... | collective-permute-start | bytes 1572872 | tf_op jit(solution)/shard_map/ppermute | solution.py:19
  239.8 4.4 %copy-start.19 = (bf16[1,1024,8,128]{1,3,2,0:T(8,128)(2,1)S(1)}, bf16[1,1024,8,128]{1,3,2,0:T(8,128)(2,1)}, u32[]{:S(2)}) copy-start(bf16[1,1024,8,128]{1,3,2,0:T(8,128)(2,1)} %get-tuple-element.52) | copy-start | bytes 6291460
  244.2 3.4 copy-start.23
  255.1 3.2 copy-start
  329.7 4.5 %copy-start.2 = (f32[1,1024,1024]{2,0,1:T(1,128)S(1)}, f32[1,1024,1024]{2,0,1:T(1,128)}, u32[]{:S(2)}) copy-start(f32[1,1024,1024]{2,0,1:T(1,128)} %get-tuple-element.53) | copy-start | bytes 12582916
Sparse Core Ops, SparseCore 0:
  248.6 72.5 all-reduce.2
where the time goes:
time: 356 us; the launch traced here: 351 us
  blocking collectives  106 us (30%)
  local copies, waits for them, and re-layouts  93.1 us (26%)
  matrix products  45.6 us (13%)
  waiting for transfers between devices  43.7 us (12%)
  other arithmetic  36.4 us (10%)
  between operations  15 us (4%)
  starting transfers between devices  10.9 us (3%)
    psum x1, blocking collectives, per_device(): gain_total = lax.psum(gain_part, ('dp', 'ctx'))  44.9 us
    psum x1, waiting for transfers between devices, per_device(): whole_dk, whole_dv = lax.psum((sum_dk, sum_dv), 'ctx')  43.6 us
    unnamed x69, local copies, waits for them, and re-layouts  31.7 us
    all_gather x1, blocking collectives, per_device(): lax.all_gather(own_sum_keys, 'ctx', axis=1, tiled=True)  30.6 us
    all_gather x1, blocking collectives, per_device(): lax.all_gather(own_sum_values, 'ctx', axis=1, tiled=True)  30.5 us
    convert_element_type x2, other arithmetic, fold_band(): return folded.reshape(batch, length, width).astype(bf16)  11.9 us
    ppermute x4, starting transfers between devices, from_behind(): lax.ppermute(value, axis, [(source, source + steps) for source in range(f...  10.9 us
    add x2, other arithmetic, fold_band(): folded = (pairs[:, :, BLOCK:] + later).reshape(batch, segs, STRIDE, width)  10.8 us
  transfers between devices with their start and end apart: 5, of which 1 were waited for; matrix products, arithmetic and copies ran while one was open for 22% of the time, Pallas kernels for 0%

commit v1 on v0

v1 whole, which is shorter than its diff:
```python
import functools

import jax
import jax.numpy as jnp
from jax import lax
from jax.experimental import pallas as pl
from jax.experimental.pallas import tpu as pltpu
from jax.sharding import PartitionSpec as P


H = 8
HD = 128
BLOCK = 128
STRIDE = 1024
SUMMARY = 8
NEG = -1e30
SCALE = HD**-0.5
EXP2_SCALE = SCALE * 1.4426950408889634

f32 = jnp.float32
bf16 = jnp.bfloat16


def from_behind(value, axis, steps):
    count = lax.axis_size(axis)
    first, last = (max(0, -steps), min(count, count - steps))
    return lax.ppermute(value, axis, [(source, source + steps) for source in range(first, last)])


def nt(a, b):
    return lax.dot_general(a, b, (((1,), (1,)), ((), ())), preferred_element_type=f32)


def nn(a, b):
    return lax.dot_general(a, b, (((1,), (0,)), ((), ())), preferred_element_type=f32)


def unpack_sums(ref):
    wide = ref[...].astype(f32)
    sources, both, width = wide.shape
    own = both // 2
    keys = wide[:, :own].reshape(sources * own, width)
    values = wide[:, own:].reshape(sources * own, width)
    return keys.astype(bf16), values.astype(bf16)


def sum_bias(total_sums, segment, first_block):
    slot = lax.broadcasted_iota(jnp.int32, (total_sums, BLOCK), 0)
    query = lax.broadcasted_iota(jnp.int32, (total_sums, BLOCK), 1)
    position = slot // SUMMARY * STRIDE + STRIDE - SUMMARY + slot % SUMMARY
    start = segment * STRIDE + (0 if first_block else BLOCK)
    return jnp.where(start + query - position >= BLOCK, 0.0, NEG).astype(f32)


def block_probs(keys2, values2, sum_keys, sum_values, scaled, grads, bias, tri, no_prev):
    s = nt(keys2, scaled)
    ss = nt(sum_keys, scaled) + bias
    dp = nt(values2, grads)
    dps = nt(sum_values, grads)
    prev = s[:BLOCK]
    if no_prev is not None:
        prev = jnp.where(no_prev, NEG, prev)
    sm = jnp.where(tri, s[BLOCK:], prev)
    dpm = jnp.where(tri, dp[BLOCK:], dp[:BLOCK])
    top = jnp.maximum(jnp.max(sm, 0, keepdims=True), jnp.max(ss, 0, keepdims=True))
    e = jnp.exp2((sm - top) * EXP2_SCALE)
    es = jnp.exp2((ss - top) * EXP2_SCALE)
    total = jnp.sum(e, 0, keepdims=True) + jnp.sum(es, 0, keepdims=True)
    inv = 1.0 / total
    p = e * inv
    ps = es * inv
    delta = jnp.sum(p * dpm, 0, keepdims=True) + jnp.sum(ps * dps, 0, keepdims=True)
    pb = p.astype(bf16)
    psb = ps.astype(bf16)
    ds = p * (dpm - delta) * SCALE
    dss = ps * (dps - delta) * SCALE
    return pb, psb, ds.astype(bf16), dss.astype(bf16)


def rim_kernel(segs, rank_ref, q, k, v, g, rim, sums, gain, out):
    rank = rank_ref[0]
    total_sums = sums.shape[0] * (sums.shape[1] // 2)
    bias = sum_bias(total_sums, rank * segs, True)
    key_at = lax.broadcasted_iota(jnp.int32, (BLOCK, BLOCK), 0)
    query_at = lax.broadcasted_iota(jnp.int32, (BLOCK, BLOCK), 1)
    tri = key_at <= query_at
    zero = jnp.zeros((BLOCK, BLOCK), bf16)
    for h in range(H):
        cols = slice(h * HD, (h + 1) * HD)
        sk, sv = unpack_sums(sums.at[:, :, cols])
        scaled = (q[:, cols].astype(f32) * gain[:, cols]).astype(bf16)
        grads = g[:, cols]
        keys2 = jnp.concatenate([rim[:BLOCK, cols], k[:, cols]], 0)
        values2 = jnp.concatenate([rim[BLOCK:, cols], v[:, cols]], 0)
        pb, _, ds, _ = block_probs(keys2, values2, sk, sv, scaled, grads, bias, tri, rank == 0)
        out[:BLOCK, cols] = nn(jnp.where(tri, zero, ds), scaled).astype(bf16)
        out[BLOCK:, cols] = nn(jnp.where(tri, zero, pb), grads).astype(bf16)


def main_kernel(
    segs, rank_ref, q, k, v, g, rim, sums, gain,
    att, gq, gk, gv, tails, sum_grads, gain_part,
    kx, vx, sc, bias_ref,
):
    rank = rank_ref[0]
    sources, both, _ = sums.shape
    total_sums = sources * both // 2
    blocks = q.shape[0] // BLOCK
    per_seg = STRIDE // BLOCK

    @pl.when(pl.program_id(0) == 0)
    def _():
        for seg in range(segs):
            bias_ref[2 * seg] = sum_bias(total_sums, rank * segs + seg, True)
            bias_ref[2 * seg + 1] = sum_bias(total_sums, rank * segs + seg, False)

    key_at = lax.broadcasted_iota(jnp.int32, (BLOCK, BLOCK), 0)
    query_at = lax.broadcasted_iota(jnp.int32, (BLOCK, BLOCK), 1)
    tri = key_at <= query_at
    low = query_at <= key_at
    zero = jnp.zeros((BLOCK, BLOCK), bf16)
    kx[:BLOCK] = rim[:BLOCK]
    kx[BLOCK:] = k[...]
    vx[:BLOCK] = rim[BLOCK:]
    vx[BLOCK:] = v[...]
    gain_row = gain[...]
    sc[...] = (q[...].astype(f32) * gain_row).astype(bf16)
    sk, sv = unpack_sums(sums)
    gain_sum = jnp.zeros((1, HD), f32)
    sum_dk = jnp.zeros((total_sums, HD), f32)
    sum_dv = jnp.zeros((total_sums, HD), f32)
    p_own = ds_own = None
    for b in range(blocks):
        rows = slice(b * BLOCK, (b + 1) * BLOCK)
        two = slice(b * BLOCK, (b + 2) * BLOCK)
        back = slice((b - 1) * BLOCK, (b + 1) * BLOCK)
        scaled = sc[rows]
        grads = g[rows]
        bias = bias_ref[2 * (b // per_seg) + (0 if b % per_seg == 0 else 1)]
        pb, psb, ds, dss = block_probs(
            kx[two], vx[two], sk, sv, scaled, grads, bias, tri, rank == 0 if b == 0 else None
        )
        sum_dv = sum_dv + nn(psb, grads)
        sum_dk = sum_dk + nn(dss, scaled)
        if b > 0:
            before = slice((b - 1) * BLOCK, b * BLOCK)
            dv = nn(jnp.concatenate([p_own, jnp.where(tri, zero, pb)], 1), g[back])
            dk = nn(jnp.concatenate([ds_own, jnp.where(tri, zero, ds)], 1), sc[back])
            if b % per_seg == 0:
                at = (b // per_seg - 1) * 2 * BLOCK
                tails[at : at + BLOCK] = dk
                tails[at + BLOCK : at + 2 * BLOCK] = dv
            else:
                gk[before] = dk.astype(bf16)
                gv[before] = dv.astype(bf16)
        p_own = jnp.where(tri, pb, zero)
        ds_own = jnp.where(tri, ds, zero)
        pt = pb.T
        dst = ds.T
        pcat = jnp.concatenate([jnp.where(low, zero, pt), jnp.where(low, pt, zero)], 1)
        o = nn(pcat, vx[two]) + nn(psb.T, sv)
        att[rows] = o.astype(bf16)
        dcat = jnp.concatenate([jnp.where(low, zero, dst), jnp.where(low, dst, zero)], 1)
        dq = nn(dcat, kx[two]) + nn(dss.T, sk)
        gq[rows] = (dq * gain_row).astype(bf16)
        gain_sum = gain_sum + jnp.sum(dq * q[rows].astype(f32), 0, keepdims=True)
    at = (segs - 1) * 2 * BLOCK
    tails[at : at + BLOCK] = nn(ds_own, scaled)
    tails[at + BLOCK : at + 2 * BLOCK] = nn(p_own, grads)
    own = both // 2
    sum_grads[...] = jnp.concatenate(
        [sum_dk.reshape(sources, own, HD), sum_dv.reshape(sources, own, HD)], 1
    ).astype(bf16)
    gain_part[...] = gain_sum


def finish_kernel(segs, gk_in, gv_in, tails, rim, sums, gk, gv):
    del gk_in, gv_in
    seg = pl.program_id(0)
    last = seg == segs - 1
    dk = tails[:BLOCK]
    dv = tails[BLOCK:]
    rim_dk = rim[:BLOCK].astype(f32)
    rim_dv = rim[BLOCK:].astype(f32)
    if segs > 1:
        rim_dk = jnp.where(last, rim_dk, 0.0)
        rim_dv = jnp.where(last, rim_dv, 0.0)
    total = jnp.sum(sums[...].astype(f32), 0)
    own = segs * SUMMARY
    body = BLOCK - SUMMARY
    dk = dk + rim_dk
    dv = dv + rim_dv
    sk = total[:SUMMARY]
    sv = total[own : own + SUMMARY]
    for other in range(1, segs):
        at = other * SUMMARY
        sk = jnp.where(seg == other, total[at : at + SUMMARY], sk)
        sv = jnp.where(seg == other, total[own + at : own + at + SUMMARY], sv)
    gk[...] = jnp.concatenate([dk[:body], dk[body:] + sk], 0).astype(bf16)
    gv[...] = jnp.concatenate([dv[:body], dv[body:] + sv], 0).astype(bf16)


def per_device(queries, keys, values, cotangent, gain):
    batch, length, width = queries.shape
    segs = length // STRIDE
    own = segs * SUMMARY
    n = lax.axis_size("ctx")
    rank = lax.axis_index("ctx")
    total_sums = n * own
    q, k, v, g = (a.reshape(length, width) for a in (queries, keys, values, cotangent))
    gain_row = gain.reshape(1, width)
    rank1 = rank.reshape(1).astype(jnp.int32)

    rim = from_behind(
        jnp.concatenate([k[length - BLOCK :], v[length - BLOCK :]], 0), "ctx", 1
    )
    own_keys = k.reshape(segs, STRIDE, width)[:, STRIDE - SUMMARY :].reshape(own, width)
    own_values = v.reshape(segs, STRIDE, width)[:, STRIDE - SUMMARY :].reshape(own, width)
    own_both = jnp.concatenate([own_keys, own_values], 0)
    sums = lax.all_to_all(jnp.broadcast_to(own_both[None], (n, 2 * own, width)), "ctx", 0, 0)

    smem = pl.BlockSpec(memory_space=pltpu.SMEM)
    first = pl.BlockSpec((BLOCK, width), lambda i: (0, 0))
    whole = lambda *shape: pl.BlockSpec(shape, lambda i: (0,) * len(shape))
    rim_grads = pl.pallas_call(
        functools.partial(rim_kernel, segs),
        grid=(1,),
        in_specs=[smem, first, first, first, first, whole(2 * BLOCK, width),
                  whole(n, 2 * own, width), whole(1, width)],
        out_specs=whole(2 * BLOCK, width),
        out_shape=jax.ShapeDtypeStruct((2 * BLOCK, width), bf16),
        cost_estimate=pl.CostEstimate(flops=500_000_000, bytes_accessed=3 << 20, transcendentals=0),
        name="rim_grads",
    )(rank1, q, k, v, g, rim, sums, gain_row)
    received = from_behind(rim_grads, "ctx", -1)
    q, rim_grads = lax.optimization_barrier((q, rim_grads))

    col = lambda rows: pl.BlockSpec((rows, HD), lambda h: (0, h))
    col3 = pl.BlockSpec((n, 2 * own, HD), lambda h: (0, 0, h))
    big = jax.ShapeDtypeStruct((length, width), bf16)
    main = pl.pallas_call(
        functools.partial(main_kernel, segs),
        grid=(H,),
        in_specs=[smem, col(length), col(length), col(length), col(length), col(2 * BLOCK),
                  col3, col(1)],
        out_specs=[col(length)] * 4 + [col(segs * 2 * BLOCK), col3, col(1)],
        out_shape=[big] * 4 + [
            jax.ShapeDtypeStruct((segs * 2 * BLOCK, width), f32),
            jax.ShapeDtypeStruct((n, 2 * own, width), bf16),
            jax.ShapeDtypeStruct((1, width), f32),
        ],
        scratch_shapes=[
            pltpu.VMEM((length + BLOCK, HD), bf16),
            pltpu.VMEM((length + BLOCK, HD), bf16),
            pltpu.VMEM((length, HD), bf16),
            pltpu.VMEM((2 * segs, total_sums, BLOCK), f32),
        ],
        cost_estimate=pl.CostEstimate(
            flops=4_000_000_000, bytes_accessed=18 << 20, transcendentals=2_000_000
        ),
        name="band_and_sums",
    )
    att, gq, gk, gv, tails, sum_grads, gain_part = main(
        rank1, q, k, v, g, rim, sums, gain_row
    )

    gain_dp = lax.psum(gain_part, "dp")
    high = gain_dp.astype(bf16)
    low = (gain_dp - high.astype(f32)).astype(bf16)
    gain_rows = jnp.concatenate([high, low], 0)
    payload = jnp.concatenate(
        [sum_grads, jnp.broadcast_to(gain_rows[None], (n, 2, width))], 1
    )
    got = lax.all_to_all(payload, "ctx", 0, 0)
    token_count = batch * lax.axis_size("dp") * length * n
    gain_grad = jnp.sum(got[:, 2 * own :].astype(f32), (0, 1)) * token_count**-0.5
    got_sums = got[:, : 2 * own]

    per_seg = STRIDE // BLOCK
    tail_spec = pl.BlockSpec((2 * BLOCK, width), lambda s: (s, 0))
    last_block = pl.BlockSpec((BLOCK, width), lambda s: (s * per_seg + per_seg - 1, 0))
    raw = pl.BlockSpec(memory_space=pl.ANY)
    gk, gv = pl.pallas_call(
        functools.partial(finish_kernel, segs),
        grid=(segs,),
        in_specs=[raw, raw, tail_spec, whole(2 * BLOCK, width), whole(n, 2 * own, width)],
        out_specs=[last_block, last_block],
        out_shape=[big, big],
        input_output_aliases={0: 0, 1: 1},
        cost_estimate=pl.CostEstimate(flops=1_000_000, bytes_accessed=3 << 20, transcendentals=0),
        name="finish",
    )(gk, gv, tails, received, got_sums)
    return (
        att.reshape(queries.shape), gq.reshape(queries.shape), gk.reshape(queries.shape),
        gv.reshape(queries.shape), gain_grad,
    )


def solution(mesh):
    spec = P("dp", "ctx", None)
    return jax.shard_map(
        per_device, mesh=mesh, in_specs=(spec,) * 4 + (P(),), out_specs=(spec,) * 4 + (P(),),
        check_vma=False,
    )
```

time: 356 us -> 93.2 us (0.26)
  the two profiles are of different devices: /device:TPU:0 before, /device:TPU:14 now
where the time goes in v1:
time: 93.2 us; the launch traced here: 92.6 us
  Pallas kernels  32.4 us (35%)
  waiting for transfers between devices  28.1 us (30%)
  starting transfers between devices  18.1 us (19%)
  blocking collectives  6.01 us (6%)
  local copies, waits for them, and re-layouts  4.97 us (5%)
  other arithmetic  2.46 us (3%)
    pallas_call x1, Pallas kernels, per_device(): main(rank1, q, k, v, g, rim, sums, gain_row)  25.5 us
    ppermute x2, waiting for transfers between devices, from_behind(): lax.ppermute(value, axis, [(source, source + steps) for source in range(f...  10.6 us
    all_to_all x1, waiting for transfers between devices, per_device(): lax.all_to_all(jnp.broadcast_to(own_both[None], (n, 2 * own, width)), 'ct...  10.6 us
    all_to_all x1, starting transfers between devices, per_device(): got = lax.all_to_all(payload, 'ctx', 0, 0)  6.92 us
    all_to_all x1, waiting for transfers between devices, per_device(): got = lax.all_to_all(payload, 'ctx', 0, 0)  6.9 us
    psum x1, blocking collectives, per_device(): gain_dp = lax.psum(gain_part, 'dp')  6.01 us
    ppermute x2, starting transfers between devices, from_behind(): lax.ppermute(value, axis, [(source, source + steps) for source in range(f...  5.92 us
    all_to_all x1, starting transfers between devices, per_device(): lax.all_to_all(jnp.broadcast_to(own_both[None], (n, 2 * own, width)), 'ct...  5.24 us
  transfers between devices with their start and end apart: 4, of which 3 were waited for; matrix products, arithmetic and copies ran while one was open for 3% of the time, Pallas kernels for 0%

profile of v1, /device:TPU:14, one launch (start us, length us, event | category | flops | bytes accessed | tf_op | source)
XLA Modules:
  0.0 92.6 jit_solution(12342944971714678912)
XLA Ops:
  0.6 1.1 %slice_bitcast_fusion = (bf16[128,1024]{1,0:T(8,128)(2,1)S(1)}, bf16[128,1024]{1,0:T(8,128)(2,1)S(1)}) fusion(bf16[1,1024,1024]{2,1,0:T(8,128)(2,1)} %param.7, bf16[1,1024,1024]{2,1,0:T(8,128)(2,1)} %param.6), kind=kLoop, calls=%fused_computation.2 | loop fusion | bytes 1048576 | tf_op jit(solution)/shard_map/slice | solution.py:215
  1.7 3.5 %collective-permute-start = (bf16[256,1024]{1,0:T(8,128)(2,1)S(1)}, bf16[256,1024]{1,0:T(8,128)(2,1)S(1)}, u32[]{:S(2)}, u32[]{:S(2)}) collective-permute-start(bf16[256,1024]{1,0:T(8,128)(2,1)S(1)} %pad_maximum_fusion), channel_id=1, source_target_pairs={{0,1},{1,2},{2,3},{3,4},{4,5},{5,6},{6,7},{8,9},{9,10},{10,11},{11... | collective-permute-start | bytes 1572872 | tf_op jit(solution)/shard_map/ppermute | solution.py:27
  5.2 0.7 slice_bitcast_fusion.2
  6.0 0.7 broadcast_in_dim.4
  6.7 5.2 %all-to-all-start = ((bf16[8,16,1024]{2,1,0:T(8,128)(2,1)}), bf16[8,16,1024]{2,1,0:T(8,128)(2,1)S(1)}, u32[]{:S(2)}, u32[]{:S(2)}) async-start(bf16[8,16,1024]{2,1,0:T(8,128)(2,1)} %broadcast_in_dim.4), calls=%async_computation | async-start | bytes 524288 | tf_op jit(solution)/shard_map/all_to_all | solution.py:220
  11.9 10.6 %all-to-all-done.sums = bf16[8,16,1024]{2,1,0:T(8,128)(2,1)S(1)} async-done(((bf16[8,16,1024]{2,1,0:T(8,128)(2,1)}), bf16[8,16,1024]{2,1,0:T(8,128)(2,1)S(1)}, u32[]{:S(2)}, u32[]{:S(2)}) %all-to-all-start) | async-done | bytes 262176 | tf_op jit(solution)/shard_map/all_to_all | solution.py:220
  22.5 0.0 copy-start
  22.5 0.0 collective-permute-done.rim
  22.5 0.0 copy-start.2
  22.5 0.7 copy-done
  23.2 0.2 copy-done.2
  23.4 4.6 %rim_grads.1 = bf16[256,1024]{1,0:T(8,128)(2,1)} custom-call(s32[1]{0:T(128)} %bitcast.rank_ref, bf16[1024,1024]{1,0:T(8,128)(2,1)} %bitcast.24, bf16[1024,1024]{1,0:T(8,128)(2,1)} %bitcast.18, bf16[1024,1024]{1,0:T(8,128)(2,1)} %bitcast.20, bf16[1024,1024]{1,0:T(8,128)(2,1)} %bitcast.26, bf16[256,1024]{1,0:T(8,128)(2,1)} %copy-done.2, ...), custom_call_target="tpu_custom_call" | custom-call | flops 500000000 | bytes 3145728 | tf_op jit(solution)/shard_map/rim_grads/pallas_call | solution.py:225
  27.9 0.0 copy-start.1
  27.9 25.5 %band_and_sums.1 = (bf16[1024,1024]{1,0:T(8,128)(2,1)}, bf16[1024,1024]{1,0:T(8,128)(2,1)}, bf16[1024,1024]{1,0:T(8,128)(2,1)}, bf16[1024,1024]{1,0:T(8,128)(2,1...) custom-call(s32[1]{0:T(128)} %bitcast.rank_ref, bf16[1024,1024]{1,0:T(8,128)(2,1)} %bitcast.25, ...), custom_call_target="tpu_custom_call" | custom-call | flops 4000000000 | bytes 18874368 | tf_op jit(solution)/shard_map/band_and_sums/pallas_call | solution.py:263
  53.5 6.0 %psum.7 = f32[1,1024]{1,0:T(1,128)S(1)} all-reduce(f32[1,1024]{1,0:T(1,128)} %get-tuple-element.22), channel_id=1, replica_groups=mesh['dp'=4,'ctx'=8] {'dp'}, use_global_device_ids=true, to_apply=%region_0.0 | all-reduce | flops 1024 | bytes 8192 | tf_op jit(solution)/shard_map/psum | solution.py:267
  59.5 1.8 %pad_maximum_fusion.1 = bf16[8,18,1024]{2,1,0:T(8,128)(2,1)} fusion(bf16[8,2,1024]{2,1,0:T(2,128)(2,1)S(1)} %broadcast_in_dim.5, bf16[8,16,1024]{2,1,0:T(8,128)(2,1)} %get-tuple-element.21), kind=kLoop, calls=%fused_computation.1 | loop fusion | flops 589824 | bytes 589824 | tf_op jit(solution)/shard_map/concatenate | solution.py:271
  61.3 6.9 %all-to-all-start.1 = ((bf16[8,18,1024]{2,1,0:T(8,128)(2,1)}), bf16[8,18,1024]{2,1,0:T(8,128)(2,1)S(1)}, u32[]{:S(2)}, u32[]{:S(2)}) async-start(bf16[8,18,1024]{2,1,0:T(8,128)(2,1)} %pad_maximum_fusion.1), calls=%async_computation.1 | async-start | bytes 786432 | tf_op jit(solution)/shard_map/all_to_all | solution.py:274
  68.2 0.0 copy-done.1
  68.2 2.5 %collective-permute-start.1 = (bf16[256,1024]{1,0:T(8,128)(2,1)S(1)}, bf16[256,1024]{1,0:T(8,128)(2,1)S(1)}, u32[]{:S(2)}, u32[]{:S(2)}) collective-permute-start(bf16[256,1024]{1,0:T(8,128)(2,1)S(1)} %copy-done.1), channel_id=1, source_target_pairs={{1,0},{2,1},{3,2},{4,3},{5,4},{6,5},{7,6},{9,8},{10,9},{11,10},{12... | collective-permute-start | bytes 1572872 | tf_op jit(solution)/shard_map/ppermute | solution.py:27
  70.7 6.9 %all-to-all-done.1 = bf16[8,18,1024]{2,1,0:T(8,128)(2,1)S(1)} async-done(((bf16[8,18,1024]{2,1,0:T(8,128)(2,1)}), bf16[8,18,1024]{2,1,0:T(8,128)(2,1)S(1)}, u32[]{:S(2)}, u32[]{:S(2)}) %all-to-all-start.1) | async-done | bytes 294944 | tf_op jit(solution)/shard_map/all_to_all | solution.py:274
  77.6 0.7 slice.32.sums
  78.3 0.6 broadcast_multiply_fusion
  78.9 10.6 %collective-permute-done.1.rim = bf16[256,1024]{1,0:T(8,128)(2,1)S(1)} collective-permute-done((bf16[256,1024]{1,0:T(8,128)(2,1)S(1)}, bf16[256,1024]{1,0:T(8,128)(2,1)S(1)}, u32[]{:S(2)}, u32[]{:S(2)}) %collective-permute-start.1) | collective-permute-done | bytes 524320 | tf_op jit(solution)/shard_map/ppermute | solution.py:27
  89.5 0.0 copy-start.3
  89.5 0.8 copy-done.3
  90.4 2.3 %finish.1 = (bf16[1024,1024]{1,0:T(8,128)(2,1)}, bf16[1024,1024]{1,0:T(8,128)(2,1)}) custom-call(bf16[1024,1024]{1,0:T(8,128)(2,1)} %get-tuple-element.18.gk_in, bf16[1024,1024]{1,0:T(8,128)(2,1)} %get-tuple-element.19.gv_in, f32[256,1024]{1,0:T(8,128)} %get-tuple-element.20.tails, ...), custom_call_target="tpu_custom_call", output_to_operand_aliasing={{0}: (0, {}), {1}: (1, {})} | custom-call | flops 1000000 | bytes 3145728 | tf_op jit(solution)/shard_map/finish/pallas_call | solution.py:283
  (6 shorter events, 0.1 us)
Async XLA Ops:
  1.7 20.7 %collective-permute-start = (bf16[256,1024]{1,0:T(8,128)(2,1)S(1)}, bf16[256,1024]{1,0:T(8,128)(2,1)S(1)}, u32[]{:S(2)}, u32[]{:S(2)}) collective-permute-start(bf16[256,1024]{1,0:T(8,128)(2,1)S(1)} %pad_maximum_fusion), channel_id=1, source_target_pairs={{0,1},{1,2},{2,3},{3,4},{4,5},{5,6},{6,7},{8,9},{9,10},{10,11},{11... | collective-permute-start | bytes 1572872 | tf_op jit(solution)/shard_map/ppermute | solution.py:27
  6.7 15.8 %all-to-all-start = ((bf16[8,16,1024]{2,1,0:T(8,128)(2,1)}), bf16[8,16,1024]{2,1,0:T(8,128)(2,1)S(1)}, u32[]{:S(2)}, u32[]{:S(2)}) async-start(bf16[8,16,1024]{2,1,0:T(8,128)(2,1)} %broadcast_in_dim.4), calls=%async_computation | async-start | bytes 524288 | tf_op jit(solution)/shard_map/all_to_all | solution.py:220
  22.5 0.7 copy-start
  22.5 0.9 copy-start.2
  27.9 40.3 %copy-start.1 = (bf16[256,1024]{1,0:T(8,128)(2,1)S(1)}, bf16[256,1024]{1,0:T(8,128)(2,1)}, u32[]{:S(2)}) copy-start(bf16[256,1024]{1,0:T(8,128)(2,1)} %rim_grads.1) | copy-start | bytes 1572868
  61.3 16.3 %all-to-all-start.1 = ((bf16[8,18,1024]{2,1,0:T(8,128)(2,1)}), bf16[8,18,1024]{2,1,0:T(8,128)(2,1)S(1)}, u32[]{:S(2)}, u32[]{:S(2)}) async-start(bf16[8,18,1024]{2,1,0:T(8,128)(2,1)} %pad_maximum_fusion.1), calls=%async_computation.1 | async-start | bytes 786432 | tf_op jit(solution)/shard_map/all_to_all | solution.py:274
  68.2 21.3 %collective-permute-start.1 = (bf16[256,1024]{1,0:T(8,128)(2,1)S(1)}, bf16[256,1024]{1,0:T(8,128)(2,1)S(1)}, u32[]{:S(2)}, u32[]{:S(2)}) collective-permute-start(bf16[256,1024]{1,0:T(8,128)(2,1)S(1)} %copy-done.1), channel_id=1, source_target_pairs={{1,0},{2,1},{3,2},{4,3},{5,4},{6,5},{7,6},{9,8},{10,9},{11,10},{12... | collective-permute-start | bytes 1572872 | tf_op jit(solution)/shard_map/ppermute | solution.py:27
  89.5 0.8 copy-start.3

commit v2 on v1

v2 whole, which is shorter than its diff:
```python
import functools

import jax
import jax.numpy as jnp
from jax import lax
from jax.experimental import pallas as pl
from jax.experimental.pallas import tpu as pltpu
from jax.sharding import PartitionSpec as P


H = 8
HD = 128
BLOCK = 128
STRIDE = 1024
SUMMARY = 8
NEG = -1e30
SCALE = HD**-0.5
EXP2_SCALE = SCALE * 1.4426950408889634

f32 = jnp.float32
bf16 = jnp.bfloat16


def from_behind(value, axis, steps):
    count = lax.axis_size(axis)
    first, last = (max(0, -steps), min(count, count - steps))
    return lax.ppermute(value, axis, [(source, source + steps) for source in range(first, last)])


def nt(a, b):
    return lax.dot_general(a, b, (((1,), (1,)), ((), ())), preferred_element_type=f32)


def nn(a, b):
    return lax.dot_general(a, b, (((1,), (0,)), ((), ())), preferred_element_type=f32)


def unpack_sums(ref):
    wide = ref[...].astype(f32)
    sources, both, width = wide.shape
    own = both // 2
    keys = wide[:, :own].reshape(sources * own, width)
    values = wide[:, own:].reshape(sources * own, width)
    return keys.astype(bf16), values.astype(bf16)


def sum_bias(total_sums, segment, first_block):
    slot = lax.broadcasted_iota(jnp.int32, (total_sums, BLOCK), 0)
    query = lax.broadcasted_iota(jnp.int32, (total_sums, BLOCK), 1)
    position = slot // SUMMARY * STRIDE + STRIDE - SUMMARY + slot % SUMMARY
    start = segment * STRIDE + (0 if first_block else BLOCK)
    return jnp.where(start + query - position >= BLOCK, 0.0, NEG).astype(f32)


def pipeline(count, first, second, third):
    for step in range(count + 2):
        if step < count:
            first(step)
        if 0 <= step - 2:
            third(step - 2)
        if 0 <= step - 1 < count:
            second(step - 1)


def triangle():
    at = [lax.broadcasted_iota(jnp.int32, (BLOCK, BLOCK), axis) for axis in (0, 1)]
    return at[0] <= at[1], at[1] <= at[0]


def score(slot, s_buf, d_buf, keys2, values2, sum_keys, sum_values, scaled, grads, tri, no_prev):
    s = nt(keys2, scaled)
    prev = s[:BLOCK]
    if no_prev is not None:
        prev = jnp.where(no_prev, NEG, prev)
    s_buf[slot, :BLOCK] = jnp.where(tri, s[BLOCK:], prev)
    s_buf[slot, BLOCK:] = nt(sum_keys, scaled)
    d = nt(values2, grads)
    d_buf[slot, :BLOCK] = jnp.where(tri, d[BLOCK:], d[:BLOCK])
    d_buf[slot, BLOCK:] = nt(sum_values, grads)


def soften(slot, s_buf, d_buf, p_buf, ds_buf, bias):
    sm = s_buf[slot, :BLOCK]
    ss = s_buf[slot, BLOCK:] + bias
    top = jnp.maximum(jnp.max(sm, 0, keepdims=True), jnp.max(ss, 0, keepdims=True))
    e = jnp.exp2((sm - top) * EXP2_SCALE)
    es = jnp.exp2((ss - top) * EXP2_SCALE)
    total = jnp.sum(e, 0, keepdims=True) + jnp.sum(es, 0, keepdims=True)
    inv = 1.0 / total
    p = e * inv
    ps = es * inv
    p_buf[slot, :BLOCK] = p.astype(bf16)
    p_buf[slot, BLOCK:] = ps.astype(bf16)
    dm = d_buf[slot, :BLOCK]
    dsum = d_buf[slot, BLOCK:]
    delta = jnp.sum(p * dm, 0, keepdims=True) + jnp.sum(ps * dsum, 0, keepdims=True)
    ds_buf[slot, :BLOCK] = (p * (dm - delta) * SCALE).astype(bf16)
    ds_buf[slot, BLOCK:] = (ps * (dsum - delta) * SCALE).astype(bf16)


def spread(buf, slot, rhs_by_query, rhs_by_key, rhs_by_sum, tri, low):
    zero = jnp.zeros((BLOCK, BLOCK), bf16)
    m = buf[slot, :BLOCK]
    ms = buf[slot, BLOCK:]
    by_key = nn(
        jnp.concatenate([jnp.where(tri, zero, m), jnp.where(tri, m, zero), ms], 0), rhs_by_query
    )
    mt = m.T
    wide = jnp.concatenate([jnp.where(low, zero, mt), jnp.where(low, mt, zero)], 1)
    by_query = nn(wide, rhs_by_key) + nn(ms.T, rhs_by_sum)
    return by_key, by_query


def rim_kernel(
    segs, rank_ref, q, k, v, g, rim, sums, gain,
    att, gq, out, heads_part, sum_part, gain_part,
    s_buf, d_buf, p_buf, ds_buf, sc, sk, sv,
):
    rank = rank_ref[0]
    sources, both, _ = sums.shape
    own = both // 2
    total_sums = sources * own
    bias = sum_bias(total_sums, rank * segs, True)
    tri, low = triangle()

    def cols(h):
        return slice(h * HD, (h + 1) * HD)

    def first(h):
        at = cols(h)
        slot = h % 3
        sk[slot], sv[slot] = unpack_sums(sums.at[:, :, at])
        sc[slot] = (q[:, at].astype(f32) * gain[:, at]).astype(bf16)
        keys2 = jnp.concatenate([rim[:BLOCK, at], k[:, at]], 0)
        values2 = jnp.concatenate([rim[BLOCK:, at], v[:, at]], 0)
        score(slot, s_buf, d_buf, keys2, values2, sk[slot], sv[slot], sc[slot], g[:, at], tri,
              rank == 0)

    def second(h):
        soften(h % 3, s_buf, d_buf, p_buf, ds_buf, bias)

    def third(h):
        at = cols(h)
        slot = h % 3
        keys2 = jnp.concatenate([rim[:BLOCK, at], k[:, at]], 0)
        values2 = jnp.concatenate([rim[BLOCK:, at], v[:, at]], 0)
        dv, o = spread(p_buf, slot, g[:, at], values2, sv[slot], tri, low)
        dk, dq = spread(ds_buf, slot, sc[slot], keys2, sk[slot], tri, low)
        att[:, at] = o.astype(bf16)
        gq[:, at] = (dq * gain[:, at]).astype(bf16)
        gain_part[:, at] = jnp.sum(dq * q[:, at].astype(f32), 0, keepdims=True)
        out[:BLOCK, at] = dk[:BLOCK].astype(bf16)
        out[BLOCK:, at] = dv[:BLOCK].astype(bf16)
        heads_part[:BLOCK, at] = dk[BLOCK : 2 * BLOCK]
        heads_part[BLOCK:, at] = dv[BLOCK : 2 * BLOCK]
        sum_part[:, :own, at] = dk[2 * BLOCK :].reshape(sources, own, HD)
        sum_part[:, own:, at] = dv[2 * BLOCK :].reshape(sources, own, HD)

    pipeline(H, first, second, third)


def main_kernel(
    segs, rank_ref, q, k, v, g, sums, gain, att_in, gq_in, heads_part, sum_part, gain_in,
    att, gq, gk, gv, tails, payload,
    s_buf, d_buf, p_buf, ds_buf, sc, sk, sv, dk_acc, dv_acc, sum_dk, sum_dv, gain_part, bias_ref,
):
    rank = rank_ref[0]
    sources, both, _ = sums.shape
    own = both // 2
    total_sums = sources * own
    blocks = q.shape[0] // BLOCK
    per_seg = STRIDE // BLOCK

    @pl.when(pl.program_id(0) == 0)
    def _():
        for seg in range(segs):
            bias_ref[2 * seg] = sum_bias(total_sums, rank * segs + seg, True)
            bias_ref[2 * seg + 1] = sum_bias(total_sums, rank * segs + seg, False)

    tri, low = triangle()
    gain_row = gain[...]
    sk[...], sv[...] = unpack_sums(sums)
    att[:BLOCK] = att_in[...]
    gq[:BLOCK] = gq_in[...]
    gain_part[...] = gain_in[...]
    sum_dk[...] = sum_part[:, :own].reshape(total_sums, HD)
    sum_dv[...] = sum_part[:, own:].reshape(total_sums, HD)

    def first(i):
        b = i + 1
        rows = slice(b * BLOCK, (b + 1) * BLOCK)
        two = slice((b - 1) * BLOCK, (b + 1) * BLOCK)
        slot = i % 3
        sc[slot] = (q[rows].astype(f32) * gain_row).astype(bf16)
        score(slot, s_buf, d_buf, k[two], v[two], sk[...], sv[...], sc[slot], g[rows], tri, None)

    def second(i):
        b = i + 1
        bias = bias_ref[2 * (b // per_seg) + (0 if b % per_seg == 0 else 1)]
        soften(i % 3, s_buf, d_buf, p_buf, ds_buf, bias)

    def third(i):
        b = i + 1
        slot = i % 3
        rows = slice(b * BLOCK, (b + 1) * BLOCK)
        before = slice((b - 1) * BLOCK, b * BLOCK)
        two = slice((b - 1) * BLOCK, (b + 1) * BLOCK)
        dv, o = spread(p_buf, slot, g[rows], v[two], sv[...], tri, low)
        dk, dq = spread(ds_buf, slot, sc[slot], k[two], sk[...], tri, low)
        att[rows] = o.astype(bf16)
        gq[rows] = (dq * gain_row).astype(bf16)
        gain_part[...] += jnp.sum(dq * q[rows].astype(f32), 0, keepdims=True)
        sum_dk[...] += dk[2 * BLOCK :]
        sum_dv[...] += dv[2 * BLOCK :]
        if b == 1:
            gk[before] = (heads_part[:BLOCK] + dk[:BLOCK]).astype(bf16)
            gv[before] = (heads_part[BLOCK:] + dv[:BLOCK]).astype(bf16)
        elif b % per_seg == 0:
            at = (b // per_seg - 1) * 2 * BLOCK
            tails[at : at + BLOCK] = dk_acc[...] + dk[:BLOCK]
            tails[at + BLOCK : at + 2 * BLOCK] = dv_acc[...] + dv[:BLOCK]
        else:
            gk[before] = (dk_acc[...] + dk[:BLOCK]).astype(bf16)
            gv[before] = (dv_acc[...] + dv[:BLOCK]).astype(bf16)
        if b == blocks - 1:
            at = (segs - 1) * 2 * BLOCK
            tails[at : at + BLOCK] = dk[BLOCK : 2 * BLOCK]
            tails[at + BLOCK : at + 2 * BLOCK] = dv[BLOCK : 2 * BLOCK]
        else:
            dk_acc[...] = dk[BLOCK : 2 * BLOCK]
            dv_acc[...] = dv[BLOCK : 2 * BLOCK]

    pipeline(blocks - 1, first, second, third)
    payload[:, :both] = jnp.concatenate(
        [sum_dk[...].reshape(sources, own, HD), sum_dv[...].reshape(sources, own, HD)], 1
    ).astype(bf16)
    part = gain_part[...]
    high = part.astype(bf16)
    rest = (part - high.astype(f32)).astype(bf16)
    payload[:, both : both + 1] = jnp.broadcast_to(high[None], (sources, 1, HD))
    payload[:, both + 1 :] = jnp.broadcast_to(rest[None], (sources, 1, HD))


def finish_kernel(segs, gk_in, gv_in, tails, rim, sums, gk, gv):
    del gk_in, gv_in
    seg = pl.program_id(0)
    last = seg == segs - 1
    dk = tails[:BLOCK]
    dv = tails[BLOCK:]
    rim_dk = rim[:BLOCK].astype(f32)
    rim_dv = rim[BLOCK:].astype(f32)
    if segs > 1:
        rim_dk = jnp.where(last, rim_dk, 0.0)
        rim_dv = jnp.where(last, rim_dv, 0.0)
    total = jnp.sum(sums[...].astype(f32), 0)
    own = segs * SUMMARY
    body = BLOCK - SUMMARY
    dk = dk + rim_dk
    dv = dv + rim_dv
    sk = total[:SUMMARY]
    sv = total[own : own + SUMMARY]
    for other in range(1, segs):
        at = other * SUMMARY
        sk = jnp.where(seg == other, total[at : at + SUMMARY], sk)
        sv = jnp.where(seg == other, total[own + at : own + at + SUMMARY], sv)
    gk[...] = jnp.concatenate([dk[:body], dk[body:] + sk], 0).astype(bf16)
    gv[...] = jnp.concatenate([dv[:body], dv[body:] + sv], 0).astype(bf16)


def per_device(queries, keys, values, cotangent, gain):
    batch, length, width = queries.shape
    segs = length // STRIDE
    own = segs * SUMMARY
    n = lax.axis_size("ctx")
    rank = lax.axis_index("ctx")
    total_sums = n * own
    q, k, v, g = (a.reshape(length, width) for a in (queries, keys, values, cotangent))
    gain_row = gain.reshape(1, width)
    rank1 = rank.reshape(1).astype(jnp.int32)

    rim = from_behind(
        jnp.concatenate([k[length - BLOCK :], v[length - BLOCK :]], 0), "ctx", 1
    )
    own_keys = k.reshape(segs, STRIDE, width)[:, STRIDE - SUMMARY :].reshape(own, width)
    own_values = v.reshape(segs, STRIDE, width)[:, STRIDE - SUMMARY :].reshape(own, width)
    own_both = jnp.concatenate([own_keys, own_values], 0)
    sums = lax.all_to_all(jnp.broadcast_to(own_both[None], (n, 2 * own, width)), "ctx", 0, 0)

    smem = pl.BlockSpec(memory_space=pltpu.SMEM)
    whole = lambda *shape: pl.BlockSpec(shape, lambda i: (0,) * len(shape))
    raw = pl.BlockSpec(memory_space=pl.ANY)
    col = lambda rows: pl.BlockSpec((rows, HD), lambda h: (0, h))
    col3 = pl.BlockSpec((n, 2 * own, HD), lambda h: (0, 0, h))
    big = jax.ShapeDtypeStruct((length, width), bf16)
    wide = BLOCK + total_sums
    buffers = [
        pltpu.VMEM((3, wide, BLOCK), f32),
        pltpu.VMEM((3, wide, BLOCK), f32),
        pltpu.VMEM((3, wide, BLOCK), bf16),
        pltpu.VMEM((3, wide, BLOCK), bf16),
        pltpu.VMEM((3, BLOCK, HD), bf16),
    ]
    first = whole(BLOCK, width)
    part3 = whole(n, 2 * own, width)
    small = [
        jax.ShapeDtypeStruct((BLOCK, width), bf16),
        jax.ShapeDtypeStruct((BLOCK, width), bf16),
        jax.ShapeDtypeStruct((2 * BLOCK, width), bf16),
        jax.ShapeDtypeStruct((2 * BLOCK, width), f32),
        jax.ShapeDtypeStruct((n, 2 * own, width), f32),
        jax.ShapeDtypeStruct((1, width), f32),
    ]
    rim_call = pl.pallas_call(
        functools.partial(rim_kernel, segs),
        grid=(1,),
        in_specs=[smem] + [first] * 4 + [whole(2 * BLOCK, width), part3, whole(1, width)],
        out_specs=[first] * 2 + [whole(2 * BLOCK, width)] * 2 + [part3, whole(1, width)],
        out_shape=small,
        scratch_shapes=buffers + [
            pltpu.VMEM((3, total_sums, HD), bf16),
            pltpu.VMEM((3, total_sums, HD), bf16),
        ],
        cost_estimate=pl.CostEstimate(flops=500_000_000, bytes_accessed=5 << 20, transcendentals=0),
        name="rim_grads",
    )
    att0, gq0, rim_grads, heads_part, sum_part, gain_part = rim_call(
        rank1, q, k, v, g, rim, sums, gain_row
    )
    received = from_behind(rim_grads, "ctx", -1)

    near = pl.BlockSpec((BLOCK, HD), lambda h: (0, h))
    col3_gain = pl.BlockSpec((n, 2 * own + 2, HD), lambda h: (0, 0, h))
    main = pl.pallas_call(
        functools.partial(main_kernel, segs),
        grid=(H,),
        in_specs=[smem] + [col(length)] * 4 + [col3, col(1), near, near, col(2 * BLOCK), col3,
                  col(1)],
        out_specs=[col(length)] * 4 + [col(segs * 2 * BLOCK), col3_gain],
        out_shape=[big] * 4 + [
            jax.ShapeDtypeStruct((segs * 2 * BLOCK, width), f32),
            jax.ShapeDtypeStruct((n, 2 * own + 2, width), bf16),
        ],
        scratch_shapes=buffers + [
            pltpu.VMEM((total_sums, HD), bf16),
            pltpu.VMEM((total_sums, HD), bf16),
            pltpu.VMEM((BLOCK, HD), f32),
            pltpu.VMEM((BLOCK, HD), f32),
            pltpu.VMEM((total_sums, HD), f32),
            pltpu.VMEM((total_sums, HD), f32),
            pltpu.VMEM((1, HD), f32),
            pltpu.VMEM((2 * segs, total_sums, BLOCK), f32),
        ],
        cost_estimate=pl.CostEstimate(
            flops=4_000_000_000, bytes_accessed=18 << 20, transcendentals=2_000_000
        ),
        name="band_and_sums",
    )
    att, gq, gk, gv, tails, payload = main(
        rank1, q, k, v, g, sums, gain_row, att0, gq0, heads_part, sum_part, gain_part
    )

    got = lax.all_to_all(payload, "ctx", 0, 0)
    gain_total = jnp.sum(got[:, 2 * own :].astype(f32), (0, 1))
    rows = lax.axis_size("dp")
    step = 1
    while step < rows:
        other = lax.ppermute(gain_total, "dp", [(i, i ^ step) for i in range(rows)])
        gain_total = gain_total + other
        step *= 2
    gain_grad = gain_total * (batch * length * n * rows) ** -0.5

    per_seg = STRIDE // BLOCK
    tail_spec = pl.BlockSpec((2 * BLOCK, width), lambda s: (s, 0))
    last_block = pl.BlockSpec((BLOCK, width), lambda s: (s * per_seg + per_seg - 1, 0))
    finish = pl.pallas_call(
        functools.partial(finish_kernel, segs),
        grid=(segs,),
        in_specs=[raw, raw, tail_spec, whole(2 * BLOCK, width), whole(n, 2 * own + 2, width)],
        out_specs=[last_block, last_block],
        out_shape=[big, big],
        input_output_aliases={0: 0, 1: 1},
        cost_estimate=pl.CostEstimate(flops=1_000_000, bytes_accessed=3 << 20, transcendentals=0),
        name="finish",
    )
    gk, gv = finish(gk, gv, tails, received, got)
    return (
        att.reshape(queries.shape), gq.reshape(queries.shape), gk.reshape(queries.shape),
        gv.reshape(queries.shape), gain_grad,
    )


def solution(mesh):
    spec = P("dp", "ctx", None)
    return jax.shard_map(
        per_device, mesh=mesh, in_specs=(spec,) * 4 + (P(),), out_specs=(spec,) * 4 + (P(),),
        check_vma=False,
    )
```

time: 93.2 us -> 74 us (0.79)
  the two profiles are of different devices: /device:TPU:14 before, /device:TPU:10 now
where the time goes in v2:
time: 74 us; the launch traced here: 73.3 us
  waiting for transfers between devices  26.2 us (35%)
  Pallas kernels  21.8 us (29%)
  starting transfers between devices  19.7 us (27%)
  local copies, waits for them, and re-layouts  4.25 us (6%)
    pallas_call x1, Pallas kernels, per_device(): main(rank1, q, k, v, g, sums, gain_row, att0, gq0, heads_part, sum_part,...  14.9 us
    all_to_all x1, waiting for transfers between devices, per_device(): lax.all_to_all(jnp.broadcast_to(own_both[None], (n, 2 * own, width)), 'ct...  10.6 us
    all_to_all x1, starting transfers between devices, per_device(): got = lax.all_to_all(payload, 'ctx', 0, 0)  6.92 us
    all_to_all x1, waiting for transfers between devices, per_device(): got = lax.all_to_all(payload, 'ctx', 0, 0)  6.91 us
    ppermute x2, starting transfers between devices, from_behind(): lax.ppermute(value, axis, [(source, source + steps) for source in range(f...  5.92 us
    ppermute x2, waiting for transfers between devices, from_behind(): lax.ppermute(value, axis, [(source, source + steps) for source in range(f...  5.44 us
    all_to_all x1, starting transfers between devices, per_device(): lax.all_to_all(jnp.broadcast_to(own_both[None], (n, 2 * own, width)), 'ct...  5.24 us
    pallas_call x1, Pallas kernels, per_device(): rim_call(rank1, q, k, v, g, rim, sums, gain_row)  4.6 us
  transfers between devices with their start and end apart: 6, of which 5 were waited for; matrix products, arithmetic and copies ran while one was open for 3% of the time, Pallas kernels for 0%

profile of v2, /device:TPU:10, one launch (start us, length us, event | category | flops | bytes accessed | tf_op | source)
XLA Modules:
  0.0 73.3 jit_solution(7531751139129811493)
XLA Ops:
  0.6 1.1 %slice_bitcast_fusion = (bf16[128,1024]{1,0:T(8,128)(2,1)S(1)}, bf16[128,1024]{1,0:T(8,128)(2,1)S(1)}) fusion(bf16[1,1024,1024]{2,1,0:T(8,128)(2,1)} %param.7, bf16[1,1024,1024]{2,1,0:T(8,128)(2,1)} %param.6), kind=kLoop, calls=%fused_computation.1 | loop fusion | bytes 1048576 | tf_op jit(solution)/shard_map/slice | solution.py:282
  1.7 3.5 %collective-permute-start = (bf16[256,1024]{1,0:T(8,128)(2,1)S(1)}, bf16[256,1024]{1,0:T(8,128)(2,1)S(1)}, u32[]{:S(2)}, u32[]{:S(2)}) collective-permute-start(bf16[256,1024]{1,0:T(8,128)(2,1)S(1)} %pad_maximum_fusion), channel_id=1, source_target_pairs={{0,1},{1,2},{2,3},{3,4},{4,5},{5,6},{6,7},{8,9},{9,10},{10,11},{11... | collective-permute-start | bytes 1572872 | tf_op jit(solution)/shard_map/ppermute | solution.py:27
  5.2 0.7 %slice_bitcast_fusion.2 = (bf16[8,1024]{1,0:T(8,128)(2,1)S(1)}, bf16[8,1024]{1,0:T(8,128)(2,1)S(1)}) fusion(bf16[1,1024,1024]{2,1,0:T(8,128)(2,1)} %param.7, bf16[1,1024,1024]{2,1,0:T(8,128)(2,1)} %param.6), kind=kLoop, calls=%fused_computation.5 | loop fusion | bytes 65536 | tf_op jit(solution)/shard_map/reshape | solution.py:285
  6.0 0.7 broadcast_in_dim.2
  6.7 5.2 %all-to-all-start = ((bf16[8,16,1024]{2,1,0:T(8,128)(2,1)}), bf16[8,16,1024]{2,1,0:T(8,128)(2,1)S(1)}, u32[]{:S(2)}, u32[]{:S(2)}) async-start(bf16[8,16,1024]{2,1,0:T(8,128)(2,1)} %broadcast_in_dim.2), calls=%async_computation | async-start | bytes 524288 | tf_op jit(solution)/shard_map/all_to_all | solution.py:287
  11.9 10.6 %all-to-all-done.sums = bf16[8,16,1024]{2,1,0:T(8,128)(2,1)S(1)} async-done(((bf16[8,16,1024]{2,1,0:T(8,128)(2,1)}), bf16[8,16,1024]{2,1,0:T(8,128)(2,1)S(1)}, u32[]{:S(2)}, u32[]{:S(2)}) %all-to-all-start) | async-done | bytes 262176 | tf_op jit(solution)/shard_map/all_to_all | solution.py:287
  22.5 0.0 copy-start.1
  22.5 0.0 collective-permute-done.rim
  22.5 0.0 copy-start.3
  22.5 0.7 copy-done.1
  23.2 0.2 copy-done.3
  23.4 4.6 %rim_grads.1 = (bf16[128,1024]{1,0:T(8,128)(2,1)}, bf16[128,1024]{1,0:T(8,128)(2,1)}, bf16[256,1024]{1,0:T(8,128)(2,1)}, f32[256,1024]{1,0:T(8,128)}, f32[8,16,1024]{2,1,0:T(8,128)}, /*index=5*/f32[1,1024]{1,0:T(1,128)}) custom-call(s32[1]{0:T(128)} %bitcast.rank_ref, bf16[1024,1024]{1,0:T(8,128)(2,1)} %bitcast.24, bf16[1024,1024]{1,0:T(8,128)(2,1)} %bitcast.18, ...), custom_call_target="tpu_custom_call" | custom-call | flops 500000000 | bytes 5242880 | tf_op jit(solution)/shard_map/rim_grads/pallas_call | solution.py:326
  28.0 0.0 copy-start.4
  28.0 14.9 %band_and_sums.1 = (bf16[1024,1024]{1,0:T(8,128)(2,1)}, bf16[1024,1024]{1,0:T(8,128)(2,1)}, bf16[1024,1024]{1,0:T(8,128)(2,1)}, bf16[1024,1024]{1,0:T(8,128)(2,1...) custom-call(s32[1]{0:T(128)} %bitcast.rank_ref, bf16[1024,1024]{1,0:T(8,128)(2,1)} %bitcast.25, ...), custom_call_target="tpu_custom_call" | custom-call | flops 4000000000 | bytes 18874368 | tf_op jit(solution)/shard_map/band_and_sums/pallas_call | solution.py:358
  42.9 6.9 %all-to-all-start.1 = ((bf16[8,18,1024]{2,1,0:T(8,128)(2,1)}), bf16[8,18,1024]{2,1,0:T(8,128)(2,1)S(1)}, u32[]{:S(2)}, u32[]{:S(2)}) async-start(bf16[8,18,1024]{2,1,0:T(8,128)(2,1)} %get-tuple-element.30), calls=%async_computation.1 | async-start | bytes 786432 | tf_op jit(solution)/shard_map/all_to_all | solution.py:362
  49.8 0.0 copy-done.4
  49.8 2.5 %collective-permute-start.1 = (bf16[256,1024]{1,0:T(8,128)(2,1)S(1)}, bf16[256,1024]{1,0:T(8,128)(2,1)S(1)}, u32[]{:S(2)}, u32[]{:S(2)}) collective-permute-start(bf16[256,1024]{1,0:T(8,128)(2,1)S(1)} %copy-done.4), channel_id=1, source_target_pairs={{1,0},{2,1},{3,2},{4,3},{5,4},{6,5},{7,6},{9,8},{10,9},{11,10},{12... | collective-permute-start | bytes 1572872 | tf_op jit(solution)/shard_map/ppermute | solution.py:27
  52.3 6.9 %all-to-all-done.1.sums = bf16[8,18,1024]{2,1,0:T(8,128)(2,1)S(1)} async-done(((bf16[8,18,1024]{2,1,0:T(8,128)(2,1)}), bf16[8,18,1024]{2,1,0:T(8,128)(2,1)S(1)}, u32[]{:S(2)}, u32[]{:S(2)}) %all-to-all-start.1) | async-done | bytes 294944 | tf_op jit(solution)/shard_map/all_to_all | solution.py:362
  59.2 0.0 copy-start
  59.2 0.1 collective-permute-start.2
  59.3 1.2 %collective-permute-done.2 = f32[1024]{0:T(1024)S(1)} collective-permute-done((f32[1024]{0:T(1024)S(1)}, f32[1024]{0:T(1024)S(1)}, u32[]{:S(2)}, u32[]{:S(2)}) %collective-permute-start.2) | collective-permute-done | bytes 4128 | tf_op jit(solution)/shard_map/ppermute | solution.py:367
  60.5 1.5 %collective-permute-start.3 = (f32[1024]{0:T(1024)S(1)}, f32[1024]{0:T(1024)S(1)}, u32[]{:S(2)}, u32[]{:S(2)}) collective-permute-start(f32[1024]{0:T(1024)S(1)} %add.6), channel_id=1, source_target_pairs={{0,16},{8,24},{16,0},{24,8},{1,17},{9,25},{17,1},{25,9},{2,18},{10... | collective-permute-start | bytes 12296 | tf_op jit(solution)/shard_map/ppermute | solution.py:367
  62.0 2.1 %collective-permute-done.3 = f32[1024]{0:T(1024)S(1)} collective-permute-done((f32[1024]{0:T(1024)S(1)}, f32[1024]{0:T(1024)S(1)}, u32[]{:S(2)}, u32[]{:S(2)}) %collective-permute-start.3) | collective-permute-done | bytes 4128 | tf_op jit(solution)/shard_map/ppermute | solution.py:367
  64.1 0.6 add_multiply_fusion
  64.7 5.4 %collective-permute-done.1.rim = bf16[256,1024]{1,0:T(8,128)(2,1)S(1)} collective-permute-done((bf16[256,1024]{1,0:T(8,128)(2,1)S(1)}, bf16[256,1024]{1,0:T(8,128)(2,1)S(1)}, u32[]{:S(2)}, u32[]{:S(2)}) %collective-permute-start.1) | collective-permute-done | bytes 524320 | tf_op jit(solution)/shard_map/ppermute | solution.py:27
  70.1 0.0 copy-start.2
  70.1 0.0 copy-done
  70.1 0.8 %copy-done.2 = bf16[256,1024]{1,0:T(8,128)(2,1)} copy-done((bf16[256,1024]{1,0:T(8,128)(2,1)}, bf16[256,1024]{1,0:T(8,128)(2,1)S(1)}, u32[]{:S(2)}) %copy-start.2) | copy-done | bytes 524312
  71.0 2.3 %finish.1 = (bf16[1024,1024]{1,0:T(8,128)(2,1)}, bf16[1024,1024]{1,0:T(8,128)(2,1)}) custom-call(bf16[1024,1024]{1,0:T(8,128)(2,1)} %get-tuple-element.26.gk_in, bf16[1024,1024]{1,0:T(8,128)(2,1)} %get-tuple-element.27.gv_in, f32[256,1024]{1,0:T(8,128)} %get-tuple-element.28.tails, ...), custom_call_target="tpu_custom_call", output_to_operand_aliasing={{0}: (0, {}), {1}: (1, {})} | custom-call | flops 1000000 | bytes 3145728 | tf_op jit(solution)/shard_map/finish/pallas_call | solution.py:385
  (4 shorter events, 0.1 us)
Async XLA Ops:
  1.7 20.7 %collective-permute-start = (bf16[256,1024]{1,0:T(8,128)(2,1)S(1)}, bf16[256,1024]{1,0:T(8,128)(2,1)S(1)}, u32[]{:S(2)}, u32[]{:S(2)}) collective-permute-start(bf16[256,1024]{1,0:T(8,128)(2,1)S(1)} %pad_maximum_fusion), channel_id=1, source_target_pairs={{0,1},{1,2},{2,3},{3,4},{4,5},{5,6},{6,7},{8,9},{9,10},{10,11},{11... | collective-permute-start | bytes 1572872 | tf_op jit(solution)/shard_map/ppermute | solution.py:27
  6.7 15.8 %all-to-all-start = ((bf16[8,16,1024]{2,1,0:T(8,128)(2,1)}), bf16[8,16,1024]{2,1,0:T(8,128)(2,1)S(1)}, u32[]{:S(2)}, u32[]{:S(2)}) async-start(bf16[8,16,1024]{2,1,0:T(8,128)(2,1)} %broadcast_in_dim.2), calls=%async_computation | async-start | bytes 524288 | tf_op jit(solution)/shard_map/all_to_all | solution.py:287
  22.5 0.7 copy-start.1
  22.5 0.9 %copy-start.3 = (bf16[256,1024]{1,0:T(8,128)(2,1)}, bf16[256,1024]{1,0:T(8,128)(2,1)S(1)}, u32[]{:S(2)}) copy-start(bf16[256,1024]{1,0:T(8,128)(2,1)S(1)} %collective-permute-done.rim) | copy-start | bytes 1572868
  28.0 21.9 %copy-start.4 = (bf16[256,1024]{1,0:T(8,128)(2,1)S(1)}, bf16[256,1024]{1,0:T(8,128)(2,1)}, u32[]{:S(2)}) copy-start(bf16[256,1024]{1,0:T(8,128)(2,1)} %get-tuple-element.29) | copy-start | bytes 1572868
  42.9 16.3 %all-to-all-start.1 = ((bf16[8,18,1024]{2,1,0:T(8,128)(2,1)}), bf16[8,18,1024]{2,1,0:T(8,128)(2,1)S(1)}, u32[]{:S(2)}, u32[]{:S(2)}) async-start(bf16[8,18,1024]{2,1,0:T(8,128)(2,1)} %get-tuple-element.30), calls=%async_computation.1 | async-start | bytes 786432 | tf_op jit(solution)/shard_map/all_to_all | solution.py:362
  49.8 20.3 %collective-permute-start.1 = (bf16[256,1024]{1,0:T(8,128)(2,1)S(1)}, bf16[256,1024]{1,0:T(8,128)(2,1)S(1)}, u32[]{:S(2)}, u32[]{:S(2)}) collective-permute-start(bf16[256,1024]{1,0:T(8,128)(2,1)S(1)} %copy-done.4), channel_id=1, source_target_pairs={{1,0},{2,1},{3,2},{4,3},{5,4},{6,5},{7,6},{9,8},{10,9},{11,10},{12... | collective-permute-start | bytes 1572872 | tf_op jit(solution)/shard_map/ppermute | solution.py:27
  59.2 10.9 %copy-start = (bf16[8,18,1024]{2,1,0:T(8,128)(2,1)}, bf16[8,18,1024]{2,1,0:T(8,128)(2,1)S(1)}, u32[]{:S(2)}) copy-start(bf16[8,18,1024]{2,1,0:T(8,128)(2,1)S(1)} %all-to-all-done.1.sums) | copy-start | bytes 884740
  59.2 1.2 %collective-permute-start.2 = (f32[1024]{0:T(1024)S(1)}, f32[1024]{0:T(1024)S(1)}, u32[]{:S(2)}, u32[]{:S(2)}) collective-permute-start(f32[1024]{0:T(1024)S(1)} %convert_reduce_fusion), channel_id=1, source_target_pairs={{0,8},{8,0},{16,24},{24,16},{1,9},{9,1},{17,25},{25,17},{2,10},{10... | collective-permute-start | bytes 12296 | tf_op jit(solution)/shard_map/ppermute | solution.py:367
  60.5 3.6 %collective-permute-start.3 = (f32[1024]{0:T(1024)S(1)}, f32[1024]{0:T(1024)S(1)}, u32[]{:S(2)}, u32[]{:S(2)}) collective-permute-start(f32[1024]{0:T(1024)S(1)} %add.6), channel_id=1, source_target_pairs={{0,16},{8,24},{16,0},{24,8},{1,17},{9,25},{17,1},{25,9},{2,18},{10... | collective-permute-start | bytes 12296 | tf_op jit(solution)/shard_map/ppermute | solution.py:367
  70.1 0.8 %copy-start.2 = (bf16[256,1024]{1,0:T(8,128)(2,1)}, bf16[256,1024]{1,0:T(8,128)(2,1)S(1)}, u32[]{:S(2)}) copy-start(bf16[256,1024]{1,0:T(8,128)(2,1)S(1)} %collective-permute-done.1.rim) | copy-start | bytes 1572868

commit v3 on v2

--- a/solution.py
+++ b/solution.py
@@ -79,7 +79,7 @@
     d_buf[slot, BLOCK:] = nt(sum_values, grads)
 
 
-def soften(slot, s_buf, d_buf, p_buf, ds_buf, bias):
+def soften(slot, s_buf, d_buf, p_out, ds_out, dss_out, bias):
     sm = s_buf[slot, :BLOCK]
     ss = s_buf[slot, BLOCK:] + bias
     top = jnp.maximum(jnp.max(sm, 0, keepdims=True), jnp.max(ss, 0, keepdims=True))
@@ -89,13 +89,13 @@
     inv = 1.0 / total
     p = e * inv
     ps = es * inv
-    p_buf[slot, :BLOCK] = p.astype(bf16)
-    p_buf[slot, BLOCK:] = ps.astype(bf16)
+    p_out[:BLOCK] = p.astype(bf16)
+    p_out[BLOCK:] = ps.astype(bf16)
     dm = d_buf[slot, :BLOCK]
     dsum = d_buf[slot, BLOCK:]
     delta = jnp.sum(p * dm, 0, keepdims=True) + jnp.sum(ps * dsum, 0, keepdims=True)
-    ds_buf[slot, :BLOCK] = (p * (dm - delta) * SCALE).astype(bf16)
-    ds_buf[slot, BLOCK:] = (ps * (dsum - delta) * SCALE).astype(bf16)
+    ds_out[...] = (p * (dm - delta) * SCALE).astype(bf16)
+    dss_out[...] = (ps * (dsum - delta) * SCALE).astype(bf16)
 
 
 def spread(buf, slot, rhs_by_query, rhs_by_key, rhs_by_sum, tri, low):
@@ -137,7 +137,8 @@
               rank == 0)
 
     def second(h):
-        soften(h % 3, s_buf, d_buf, p_buf, ds_buf, bias)
+        ds = ds_buf.at[h % 3]
+        soften(h % 3, s_buf, d_buf, p_buf.at[h % 3], ds.at[:BLOCK], ds.at[BLOCK:], bias)
 
     def third(h):
         at = cols(h)
@@ -160,14 +161,15 @@
 
 
 def main_kernel(
-    segs, rank_ref, q, k, v, g, sums, gain, att_in, gq_in, heads_part, sum_part, gain_in,
-    att, gq, gk, gv, tails, payload,
-    s_buf, d_buf, p_buf, ds_buf, sc, sk, sv, dk_acc, dv_acc, sum_dk, sum_dv, gain_part, bias_ref,
+    segs, rank_ref, q, k, v, g, sums, gain, gq_in, sum_part, gain_in,
+    gq, p_out, ds_out, payload,
+    s_buf, d_buf, dss_buf, sc, sk, sv, sum_dk, sum_dv, gain_part, bias_ref,
 ):
     rank = rank_ref[0]
     sources, both, _ = sums.shape
     own = both // 2
     total_sums = sources * own
+    wide = BLOCK + total_sums
     blocks = q.shape[0] // BLOCK
     per_seg = STRIDE // BLOCK
 
@@ -178,9 +180,9 @@
             bias_ref[2 * seg + 1] = sum_bias(total_sums, rank * segs + seg, False)
 
     tri, low = triangle()
+    zero = jnp.zeros((BLOCK, BLOCK), bf16)
     gain_row = gain[...]
     sk[...], sv[...] = unpack_sums(sums)
-    att[:BLOCK] = att_in[...]
     gq[:BLOCK] = gq_in[...]
     gain_part[...] = gain_in[...]
     sum_dk[...] = sum_part[:, :own].reshape(total_sums, HD)
@@ -188,47 +190,34 @@
 
     def first(i):
         b = i + 1
+        slot = i % 3
         rows = slice(b * BLOCK, (b + 1) * BLOCK)
         two = slice((b - 1) * BLOCK, (b + 1) * BLOCK)
-        slot = i % 3
         sc[slot] = (q[rows].astype(f32) * gain_row).astype(bf16)
         score(slot, s_buf, d_buf, k[two], v[two], sk[...], sv[...], sc[slot], g[rows], tri, None)
 
     def second(i):
         b = i + 1
         bias = bias_ref[2 * (b // per_seg) + (0 if b % per_seg == 0 else 1)]
-        soften(i % 3, s_buf, d_buf, p_buf, ds_buf, bias)
+        at = i * wide
+        soften(
+            i % 3, s_buf, d_buf, p_out.at[at : at + wide], ds_out.at[i * BLOCK : b * BLOCK],
+            dss_buf.at[i % 3], bias,
+        )
 
     def third(i):
         b = i + 1
         slot = i % 3
         rows = slice(b * BLOCK, (b + 1) * BLOCK)
-        before = slice((b - 1) * BLOCK, b * BLOCK)
         two = slice((b - 1) * BLOCK, (b + 1) * BLOCK)
-        dv, o = spread(p_buf, slot, g[rows], v[two], sv[...], tri, low)
-        dk, dq = spread(ds_buf, slot, sc[slot], k[two], sk[...], tri, low)
-        att[rows] = o.astype(bf16)
+        ms = dss_buf[slot]
+        mt = ds_out[i * BLOCK : b * BLOCK].T
+        pair = jnp.concatenate([jnp.where(low, zero, mt), jnp.where(low, mt, zero)], 1)
+        dq = nn(pair, k[two]) + nn(ms.T, sk[...])
         gq[rows] = (dq * gain_row).astype(bf16)
         gain_part[...] += jnp.sum(dq * q[rows].astype(f32), 0, keepdims=True)
-        sum_dk[...] += dk[2 * BLOCK :]
-        sum_dv[...] += dv[2 * BLOCK :]
-        if b == 1:
-            gk[before] = (heads_part[:BLOCK] + dk[:BLOCK]).astype(bf16)
-            gv[before] = (heads_part[BLOCK:] + dv[:BLOCK]).astype(bf16)
-        elif b % per_seg == 0:
-            at = (b // per_seg - 1) * 2 * BLOCK
-            tails[at : at + BLOCK] = dk_acc[...] + dk[:BLOCK]
-            tails[at + BLOCK : at + 2 * BLOCK] = dv_acc[...] + dv[:BLOCK]
-        else:
-            gk[before] = (dk_acc[...] + dk[:BLOCK]).astype(bf16)
-            gv[before] = (dv_acc[...] + dv[:BLOCK]).astype(bf16)
-        if b == blocks - 1:
-            at = (segs - 1) * 2 * BLOCK
-            tails[at : at + BLOCK] = dk[BLOCK : 2 * BLOCK]
-            tails[at + BLOCK : at + 2 * BLOCK] = dv[BLOCK : 2 * BLOCK]
-        else:
-            dk_acc[...] = dk[BLOCK : 2 * BLOCK]
-            dv_acc[...] = dv[BLOCK : 2 * BLOCK]
+        sum_dk[...] += nn(ms, sc[slot])
+        sum_dv[...] += nn(p_out[i * wide + BLOCK : (i + 1) * wide], g[rows])
 
     pipeline(blocks - 1, first, second, third)
     payload[:, :both] = jnp.concatenate(
@@ -239,6 +228,63 @@
     rest = (part - high.astype(f32)).astype(bf16)
     payload[:, both : both + 1] = jnp.broadcast_to(high[None], (sources, 1, HD))
     payload[:, both + 1 :] = jnp.broadcast_to(rest[None], (sources, 1, HD))
+
+
+def own_kernel(q, v, g, p_in, ds_in, sums, gain, att_in, heads_part, att, gk, gv, tails, sc):
+    for h in range(q.shape[1] // HD):
+        at = slice(h * HD, (h + 1) * HD)
+        heads = q.shape[1] // HD
+        p_rows = p_in.shape[0] // heads
+        ds_rows = ds_in.shape[0] // heads
+        own_head(
+            q.at[:, at], v.at[:, at], g.at[:, at],
+            p_in.at[h * p_rows : (h + 1) * p_rows], ds_in.at[h * ds_rows : (h + 1) * ds_rows],
+            sums.at[:, :, at], gain.at[:, at], att_in.at[:, at], heads_part.at[:, at],
+            att.at[:, at], gk.at[:, at], gv.at[:, at], tails.at[:, at], sc.at[h],
+        )
+
+
+def own_head(q, v, g, p_in, ds_in, sums, gain, att_in, heads_part, att, gk, gv, tails, sc):
+    blocks = q.shape[0] // BLOCK
+    per_seg = STRIDE // BLOCK
+    _, sv = unpack_sums(sums)
+    wide = BLOCK + sv.shape[0]
+    tri, low = triangle()
+    zero = jnp.zeros((BLOCK, BLOCK), bf16)
+    sc[...] = (q[...].astype(f32) * gain[...]).astype(bf16)
+    att[:BLOCK] = att_in[...]
+    for b in range(blocks):
+        rows = slice(b * BLOCK, (b + 1) * BLOCK)
+        if b > 0:
+            at = (b - 1) * wide
+            p = p_in[at : at + BLOCK]
+            pt = p.T
+            pair = jnp.concatenate([jnp.where(low, zero, pt), jnp.where(low, pt, zero)], 1)
+            o = nn(pair, v[(b - 1) * BLOCK : (b + 1) * BLOCK])
+            att[rows] = (o + nn(p_in[at + BLOCK : at + wide].T, sv)).astype(bf16)
+            p_own = jnp.where(tri, p, zero)
+            ds_own = jnp.where(tri, ds_in[(b - 1) * BLOCK : rows.start], zero)
+        if b < blocks - 1:
+            p_next = jnp.where(tri, zero, p_in[b * wide : b * wide + BLOCK])
+            ds_next = jnp.where(tri, zero, ds_in[b * BLOCK : (b + 1) * BLOCK])
+        if b == 0:
+            following = slice(BLOCK, 2 * BLOCK)
+            dk = heads_part[:BLOCK] + nn(ds_next, sc[following])
+            dv = heads_part[BLOCK:] + nn(p_next, g[following])
+        elif b < blocks - 1:
+            both = slice(b * BLOCK, (b + 2) * BLOCK)
+            dk = nn(jnp.concatenate([ds_own, ds_next], 1), sc[both])
+            dv = nn(jnp.concatenate([p_own, p_next], 1), g[both])
+        else:
+            dk = nn(ds_own, sc[rows])
+            dv = nn(p_own, g[rows])
+        if b % per_seg == per_seg - 1:
+            at = b // per_seg * 2 * BLOCK
+            tails[at : at + BLOCK] = dk
+            tails[at + BLOCK : at + 2 * BLOCK] = dv
+        else:
+            gk[rows] = dk.astype(bf16)
+            gv[rows] = dv.astype(bf16)
 
 
 def finish_kernel(segs, gk_in, gv_in, tails, rim, sums, gk, gv):
@@ -330,34 +376,55 @@
 
     near = pl.BlockSpec((BLOCK, HD), lambda h: (0, h))
     col3_gain = pl.BlockSpec((n, 2 * own + 2, HD), lambda h: (0, 0, h))
+    packed = lambda rows: pl.BlockSpec((rows, HD), lambda h: (h, 0))
+    later = length // BLOCK - 1
     main = pl.pallas_call(
         functools.partial(main_kernel, segs),
         grid=(H,),
-        in_specs=[smem] + [col(length)] * 4 + [col3, col(1), near, near, col(2 * BLOCK), col3,
-                  col(1)],
-        out_specs=[col(length)] * 4 + [col(segs * 2 * BLOCK), col3_gain],
-        out_shape=[big] * 4 + [
-            jax.ShapeDtypeStruct((segs * 2 * BLOCK, width), f32),
+        in_specs=[smem] + [col(length)] * 4 + [col3, col(1), near, col3, col(1)],
+        out_specs=[col(length), packed(later * wide), packed(later * BLOCK), col3_gain],
+        out_shape=[
+            big,
+            jax.ShapeDtypeStruct((H * later * wide, HD), bf16),
+            jax.ShapeDtypeStruct((H * later * BLOCK, HD), bf16),
             jax.ShapeDtypeStruct((n, 2 * own + 2, width), bf16),
         ],
-        scratch_shapes=buffers + [
+        scratch_shapes=[
+            pltpu.VMEM((3, wide, BLOCK), f32),
+            pltpu.VMEM((3, wide, BLOCK), f32),
+            pltpu.VMEM((3, total_sums, BLOCK), bf16),
+            pltpu.VMEM((3, BLOCK, HD), bf16),
             pltpu.VMEM((total_sums, HD), bf16),
             pltpu.VMEM((total_sums, HD), bf16),
-            pltpu.VMEM((BLOCK, HD), f32),
-            pltpu.VMEM((BLOCK, HD), f32),
             pltpu.VMEM((total_sums, HD), f32),
             pltpu.VMEM((total_sums, HD), f32),
             pltpu.VMEM((1, HD), f32),
             pltpu.VMEM((2 * segs, total_sums, BLOCK), f32),
         ],
         cost_estimate=pl.CostEstimate(
-            flops=4_000_000_000, bytes_accessed=18 << 20, transcendentals=2_000_000
+            flops=2_500_000_000, bytes_accessed=16 << 20, transcendentals=2_000_000
         ),
-        name="band_and_sums",
-    )
-    att, gq, gk, gv, tails, payload = main(
-        rank1, q, k, v, g, sums, gain_row, att0, gq0, heads_part, sum_part, gain_part
-    )
+        name="soft",
+    )
+    gq, p_all, ds_all, payload = main(rank1, q, k, v, g, sums, gain_row, gq0, sum_part, gain_part)
+
+    group = 2
+    slab = lambda rows: pl.BlockSpec((rows, group * HD), lambda h: (0, h))
+    slab3 = pl.BlockSpec((n, 2 * own, group * HD), lambda h: (0, 0, h))
+    ours = pl.pallas_call(
+        own_kernel,
+        grid=(H // group,),
+        in_specs=[slab(length)] * 3 + [packed(group * later * wide), packed(group * later * BLOCK),
+                  slab3, slab(1), slab(BLOCK), slab(2 * BLOCK)],
+        out_specs=[slab(length)] * 3 + [slab(segs * 2 * BLOCK)],
+        out_shape=[big] * 3 + [jax.ShapeDtypeStruct((segs * 2 * BLOCK, width), f32)],
+        scratch_shapes=[pltpu.VMEM((group, length, HD), bf16)],
+        cost_estimate=pl.CostEstimate(
+            flops=1_500_000_000, bytes_accessed=20 << 20, transcendentals=0
+        ),
+        name="own_grads",
+    )
+    att, gk, gv, tails = ours(q, v, g, p_all, ds_all, sums, gain_row, att0, heads_part)
 
     got = lax.all_to_all(payload, "ctx", 0, 0)
     gain_total = jnp.sum(got[:, 2 * own :].astype(f32), (0, 1))

time: 74 us -> 78.1 us (1.055)
  the two profiles are of different devices: /device:TPU:10 before, /device:TPU:0 now
where the time goes in v3:
time: 78.1 us; the launch traced here: 77.3 us
  Pallas kernels  29.3 us (38%)
  starting transfers between devices  21.5 us (28%)
  waiting for transfers between devices  21 us (27%)
  local copies, waits for them, and re-layouts  4.22 us (5%)
    pallas_call x1, Pallas kernels, per_device(): main(rank1, q, k, v, g, sums, gain_row, gq0, sum_part, gain_part)  13 us
    all_to_all x1, waiting for transfers between devices, per_device(): got = lax.all_to_all(payload, 'ctx', 0, 0)  11.2 us
    pallas_call x1, Pallas kernels, per_device(): ours(q, v, g, p_all, ds_all, sums, gain_row, att0, heads_part)  9.31 us
    all_to_all x1, starting transfers between devices, per_device(): got = lax.all_to_all(payload, 'ctx', 0, 0)  8.84 us
    all_to_all x1, waiting for transfers between devices, per_device(): lax.all_to_all(jnp.broadcast_to(own_both[None], (n, 2 * own, width)), 'ct...  8.64 us
    ppermute x2, starting transfers between devices, from_behind(): lax.ppermute(value, axis, [(source, source + steps) for source in range(f...  6.2 us
    all_to_all x1, starting transfers between devices, per_device(): lax.all_to_all(jnp.broadcast_to(own_both[None], (n, 2 * own, width)), 'ct...  4.85 us
    pallas_call x1, Pallas kernels, per_device(): rim_call(rank1, q, k, v, g, rim, sums, gain_row)  4.59 us
  transfers between devices with their start and end apart: 6, of which 3 were waited for; matrix products, arithmetic and copies ran while one was open for 3% of the time, Pallas kernels for 12%

profile of v3, /device:TPU:0, one launch (start us, length us, event | category | flops | bytes accessed | tf_op | source)
XLA Modules:
  0.0 77.3 jit_solution(4379415039487626490)
XLA Ops:
  0.6 1.1 %slice_bitcast_fusion = (bf16[128,1024]{1,0:T(8,128)(2,1)S(1)}, bf16[128,1024]{1,0:T(8,128)(2,1)S(1)}) fusion(bf16[1,1024,1024]{2,1,0:T(8,128)(2,1)} %param.7, bf16[1,1024,1024]{2,1,0:T(8,128)(2,1)} %param.6), kind=kLoop, calls=%fused_computation.1 | loop fusion | bytes 1048576 | tf_op jit(solution)/shard_map/slice | solution.py:328
  1.7 4.9 %collective-permute-start = (bf16[256,1024]{1,0:T(8,128)(2,1)S(1)}, bf16[256,1024]{1,0:T(8,128)(2,1)S(1)}, u32[]{:S(2)}, u32[]{:S(2)}) collective-permute-start(bf16[256,1024]{1,0:T(8,128)(2,1)S(1)} %pad_maximum_fusion), channel_id=1, source_target_pairs={{0,1},{1,2},{2,3},{3,4},{4,5},{5,6},{6,7},{8,9},{9,10},{10,11},{11... | collective-permute-start | bytes 1572872 | tf_op jit(solution)/shard_map/ppermute | solution.py:27
  6.7 0.7 slice_bitcast_fusion.2
  7.4 0.7 broadcast_in_dim.2
  8.1 4.8 %all-to-all-start = ((bf16[8,16,1024]{2,1,0:T(8,128)(2,1)}), bf16[8,16,1024]{2,1,0:T(8,128)(2,1)S(1)}, u32[]{:S(2)}, u32[]{:S(2)}) async-start(bf16[8,16,1024]{2,1,0:T(8,128)(2,1)} %broadcast_in_dim.2), calls=%async_computation | async-start | bytes 524288 | tf_op jit(solution)/shard_map/all_to_all | solution.py:333
  13.0 8.6 %all-to-all-done.sums = bf16[8,16,1024]{2,1,0:T(8,128)(2,1)S(1)} async-done(((bf16[8,16,1024]{2,1,0:T(8,128)(2,1)}), bf16[8,16,1024]{2,1,0:T(8,128)(2,1)S(1)}, u32[]{:S(2)}, u32[]{:S(2)}) %all-to-all-start) | async-done | bytes 262176 | tf_op jit(solution)/shard_map/all_to_all | solution.py:333
  21.6 0.0 copy-start
  21.6 0.0 collective-permute-done.rim
  21.6 0.0 copy-start.3
  21.6 0.7 copy-done
  22.3 0.2 copy-done.3
  22.5 4.6 %rim_grads.1 = (bf16[128,1024]{1,0:T(8,128)(2,1)}, bf16[128,1024]{1,0:T(8,128)(2,1)}, bf16[256,1024]{1,0:T(8,128)(2,1)}, f32[256,1024]{1,0:T(8,128)}, f32[8,16,1024]{2,1,0:T(8,128)}, /*index=5*/f32[1,1024]{1,0:T(1,128)}) custom-call(s32[1]{0:T(128)} %bitcast.3.rank_ref, bf16[1024,1024]{1,0:T(8,128)(2,1)} %bitcast.21, bf16[1024,1024]{1,0:T(8,128)(2,1)} %bitcast.27, ...), custom_call_target="tpu_custom_call" | custom-call | flops 500000000 | bytes 5242880 | tf_op jit(solution)/shard_map/rim_grads/pallas_call | solution.py:372
  27.1 0.0 copy-start.4
  27.1 13.0 %soft.1 = (bf16[1024,1024]{1,0:T(8,128)(2,1)}, bf16[10752,128]{1,0:T(8,128)(2,1)}, bf16[7168,128]{1,0:T(8,128)(2,1)}, bf16[8,18,1024]{2,1,0:T(8,128)(2,1)}) custom-call(s32[1]{0:T(128)} %bitcast.3.rank_ref, bf16[1024,1024]{1,0:T(8,128)(2,1)} %bitcast.22, bf16[1024,1024]{1,0:T(8,128)(2,1)} %bitcast.28, bf16[1024,1024]{1,0:T(8,128)(2,1)} %bitcast.19, ...), custom_call_target="tpu_custom_call" | custom-call | flops 2500000000 | bytes 16777216 | tf_op jit(solution)/shard_map/soft/pallas_call | solution.py:409
  40.1 8.8 %all-to-all-start.1 = ((bf16[8,18,1024]{2,1,0:T(8,128)(2,1)}), bf16[8,18,1024]{2,1,0:T(8,128)(2,1)S(1)}, u32[]{:S(2)}, u32[]{:S(2)}) async-start(bf16[8,18,1024]{2,1,0:T(8,128)(2,1)} %get-tuple-element.34), calls=%async_computation.1 | async-start | bytes 786432 | tf_op jit(solution)/shard_map/all_to_all | solution.py:429
  49.0 0.0 copy-done.4
  49.0 1.3 %collective-permute-start.1 = (bf16[256,1024]{1,0:T(8,128)(2,1)S(1)}, bf16[256,1024]{1,0:T(8,128)(2,1)S(1)}, u32[]{:S(2)}, u32[]{:S(2)}) collective-permute-start(bf16[256,1024]{1,0:T(8,128)(2,1)S(1)} %copy-done.4), channel_id=1, source_target_pairs={{1,0},{2,1},{3,2},{4,3},{5,4},{6,5},{7,6},{9,8},{10,9},{11,10},{12... | collective-permute-start | bytes 1572872 | tf_op jit(solution)/shard_map/ppermute | solution.py:27
  50.3 11.2 %all-to-all-done.1.sums = bf16[8,18,1024]{2,1,0:T(8,128)(2,1)S(1)} async-done(((bf16[8,18,1024]{2,1,0:T(8,128)(2,1)}), bf16[8,18,1024]{2,1,0:T(8,128)(2,1)S(1)}, u32[]{:S(2)}, u32[]{:S(2)}) %all-to-all-start.1) | async-done | bytes 294944 | tf_op jit(solution)/shard_map/all_to_all | solution.py:429
  61.5 0.0 copy-start.1
  61.5 0.1 collective-permute-start.2
  61.6 1.2 %collective-permute-done.2 = f32[1024]{0:T(1024)S(1)} collective-permute-done((f32[1024]{0:T(1024)S(1)}, f32[1024]{0:T(1024)S(1)}, u32[]{:S(2)}, u32[]{:S(2)}) %collective-permute-start.2) | collective-permute-done | bytes 4128 | tf_op jit(solution)/shard_map/ppermute | solution.py:434
  62.7 1.5 %collective-permute-start.3 = (f32[1024]{0:T(1024)S(1)}, f32[1024]{0:T(1024)S(1)}, u32[]{:S(2)}, u32[]{:S(2)}) collective-permute-start(f32[1024]{0:T(1024)S(1)} %add.6), channel_id=1, source_target_pairs={{0,16},{8,24},{16,0},{24,8},{1,17},{9,25},{17,1},{25,9},{2,18},{10... | collective-permute-start | bytes 12296 | tf_op jit(solution)/shard_map/ppermute | solution.py:434
  64.3 9.3 %own_grads.1 = (bf16[1024,1024]{1,0:T(8,128)(2,1)}, bf16[1024,1024]{1,0:T(8,128)(2,1)}, bf16[1024,1024]{1,0:T(8,128)(2,1)}, f32[256,1024]{1,0:T(8,128)}) custom-call(bf16[1024,1024]{1,0:T(8,128)(2,1)} %bitcast.23, bf16[1024,1024]{1,0:T(8,128)(2,1)} %bitcast.20, bf16[1024,1024]{1,0:T(8,128)(2,1)} %bitcast.26, bf16[10752,128]{1,0:T(8,128)(2,1)} %get-tuple-element.24.p_in, ...), custom_call_target="tpu_custom_call" | custom-call | flops 1500000000 | bytes 20971520 | tf_op jit(solution)/shard_map/own_grads/pallas_call | solution.py:427
  73.6 0.0 copy-done.1
  73.6 0.0 collective-permute-done.3
  73.6 0.6 add_multiply_fusion
  74.2 0.0 collective-permute-done.1.rim
  74.2 0.0 copy-start.2
  74.2 0.8 %copy-done.2 = bf16[256,1024]{1,0:T(8,128)(2,1)} copy-done((bf16[256,1024]{1,0:T(8,128)(2,1)}, bf16[256,1024]{1,0:T(8,128)(2,1)S(1)}, u32[]{:S(2)}) %copy-start.2) | copy-done | bytes 524312
  75.0 2.3 %finish.1 = (bf16[1024,1024]{1,0:T(8,128)(2,1)}, bf16[1024,1024]{1,0:T(8,128)(2,1)}) custom-call(bf16[1024,1024]{1,0:T(8,128)(2,1)} %get-tuple-element.30.gk_in, bf16[1024,1024]{1,0:T(8,128)(2,1)} %get-tuple-element.31.gv_in, f32[256,1024]{1,0:T(8,128)} %get-tuple-element.32.tails, ...), custom_call_target="tpu_custom_call", output_to_operand_aliasing={{0}: (0, {}), {1}: (1, {})} | custom-call | flops 1000000 | bytes 3145728 | tf_op jit(solution)/shard_map/finish/pallas_call | solution.py:452
  (4 shorter events, 0.1 us)
Async XLA Ops:
  1.7 19.9 %collective-permute-start = (bf16[256,1024]{1,0:T(8,128)(2,1)S(1)}, bf16[256,1024]{1,0:T(8,128)(2,1)S(1)}, u32[]{:S(2)}, u32[]{:S(2)}) collective-permute-start(bf16[256,1024]{1,0:T(8,128)(2,1)S(1)} %pad_maximum_fusion), channel_id=1, source_target_pairs={{0,1},{1,2},{2,3},{3,4},{4,5},{5,6},{6,7},{8,9},{9,10},{10,11},{11... | collective-permute-start | bytes 1572872 | tf_op jit(solution)/shard_map/ppermute | solution.py:27
  8.1 13.5 %all-to-all-start = ((bf16[8,16,1024]{2,1,0:T(8,128)(2,1)}), bf16[8,16,1024]{2,1,0:T(8,128)(2,1)S(1)}, u32[]{:S(2)}, u32[]{:S(2)}) async-start(bf16[8,16,1024]{2,1,0:T(8,128)(2,1)} %broadcast_in_dim.2), calls=%async_computation | async-start | bytes 524288 | tf_op jit(solution)/shard_map/all_to_all | solution.py:333
  21.6 0.7 copy-start
  21.6 0.9 %copy-start.3 = (bf16[256,1024]{1,0:T(8,128)(2,1)}, bf16[256,1024]{1,0:T(8,128)(2,1)S(1)}, u32[]{:S(2)}) copy-start(bf16[256,1024]{1,0:T(8,128)(2,1)S(1)} %collective-permute-done.rim) | copy-start | bytes 1572868
  27.1 21.9 %copy-start.4 = (bf16[256,1024]{1,0:T(8,128)(2,1)S(1)}, bf16[256,1024]{1,0:T(8,128)(2,1)}, u32[]{:S(2)}) copy-start(bf16[256,1024]{1,0:T(8,128)(2,1)} %get-tuple-element.33) | copy-start | bytes 1572868
  40.1 21.3 %all-to-all-start.1 = ((bf16[8,18,1024]{2,1,0:T(8,128)(2,1)}), bf16[8,18,1024]{2,1,0:T(8,128)(2,1)S(1)}, u32[]{:S(2)}, u32[]{:S(2)}) async-start(bf16[8,18,1024]{2,1,0:T(8,128)(2,1)} %get-tuple-element.34), calls=%async_computation.1 | async-start | bytes 786432 | tf_op jit(solution)/shard_map/all_to_all | solution.py:429
  49.0 25.2 %collective-permute-start.1 = (bf16[256,1024]{1,0:T(8,128)(2,1)S(1)}, bf16[256,1024]{1,0:T(8,128)(2,1)S(1)}, u32[]{:S(2)}, u32[]{:S(2)}) collective-permute-start(bf16[256,1024]{1,0:T(8,128)(2,1)S(1)} %copy-done.4), channel_id=1, source_target_pairs={{1,0},{2,1},{3,2},{4,3},{5,4},{6,5},{7,6},{9,8},{10,9},{11,10},{12... | collective-permute-start | bytes 1572872 | tf_op jit(solution)/shard_map/ppermute | solution.py:27
  61.5 12.1 %copy-start.1 = (bf16[8,18,1024]{2,1,0:T(8,128)(2,1)}, bf16[8,18,1024]{2,1,0:T(8,128)(2,1)S(1)}, u32[]{:S(2)}) copy-start(bf16[8,18,1024]{2,1,0:T(8,128)(2,1)S(1)} %all-to-all-done.1.sums) | copy-start | bytes 884740
  61.5 1.2 %collective-permute-start.2 = (f32[1024]{0:T(1024)S(1)}, f32[1024]{0:T(1024)S(1)}, u32[]{:S(2)}, u32[]{:S(2)}) collective-permute-start(f32[1024]{0:T(1024)S(1)} %convert_reduce_fusion), channel_id=1, source_target_pairs={{0,8},{8,0},{16,24},{24,16},{1,9},{9,1},{17,25},{25,17},{2,10},{10... | collective-permute-start | bytes 12296 | tf_op jit(solution)/shard_map/ppermute | solution.py:434
  62.7 10.8 %collective-permute-start.3 = (f32[1024]{0:T(1024)S(1)}, f32[1024]{0:T(1024)S(1)}, u32[]{:S(2)}, u32[]{:S(2)}) collective-permute-start(f32[1024]{0:T(1024)S(1)} %add.6), channel_id=1, source_target_pairs={{0,16},{8,24},{16,0},{24,8},{1,17},{9,25},{17,1},{25,9},{2,18},{10... | collective-permute-start | bytes 12296 | tf_op jit(solution)/shard_map/ppermute | solution.py:434
  74.2 0.8 %copy-start.2 = (bf16[256,1024]{1,0:T(8,128)(2,1)}, bf16[256,1024]{1,0:T(8,128)(2,1)S(1)}, u32[]{:S(2)}) copy-start(bf16[256,1024]{1,0:T(8,128)(2,1)S(1)} %collective-permute-done.1.rim) | copy-start | bytes 1572868
